TPU v7x, 512 devices: a whole 4x8x8 slice. The times are simulated.
512 devices in a mesh: region: 16 (over z, core), dev: 32 (over y, x).
Axes of the slice: x: 4, y: 8, z: 8, core: 2. Of those that a mesh axis runs over, the one named last changes fastest.
Arguments:
- basis_values: bfloat16 [6144, 4, 256, 128], P(('region', 'dev')), may hold values from -6 to 6
- density_rows: bfloat16 [1536, 4, 128, 128], P(('region', 'dev')), may hold values from -0.013671875 to 0.013671875
- block_mask: int32 [1536, 4], P(('region', 'dev')), may hold values 0 or 1
- window_start: int32 [512], P(('region', 'dev')), may hold values from 0 to 95
- batch_offsets: int32 [512, 12], P(('region', 'dev')), may hold values from 0 to 28, as said below
- batch_sizes: int32 [512, 12], P(('region', 'dev')), may hold values from 1 to 256, 1920 in all within a row
- atom_near: int32 [6144, 6], P(('region', 'dev')), may hold values from 0 to 1535
- harmonics: bfloat16 [6144, 6, 25, 256], P(('region', 'dev')), may hold values from -6 to 6
- partition: float32 [6144, 6, 256], P(('region', 'dev')), may hold values from 0.002 to 0.05
- radius: float32 [6144, 6, 256], P(('region', 'dev')), may hold values from 0 to 15
- radial_table: float32 [25, 16], replicated, may hold values from -1.5 to 1.5
Outputs:
- density: float32 [6144, 256], P(('region', 'dev'))
- moments: float32 [25, 8192], P(None, ('region', 'dev'))
- potential: float32 [6144, 256], P(('region', 'dev'))
Inputs may be any that keep to these rules, and one draw needn't show every extreme that they name: The blocks of a batch are positions batch_offsets to batch_offsets + 3 of its device's window of 32 consecutive blocks.
All inputs are finite; a program needn't handle non-finite values. No bound on the sum of `block_mask` on one device may be relied on, other than what follows from the above.
Results may differ from a plain program's by a relative error of at most 0.0029.
Values may be sent and summed in bfloat16 or wider, within the bound.
A program may use at most 64 MiB of HBM per device.

v0:
```python
import jax
import jax.numpy as jnp
from jax import lax
from jax.sharding import PartitionSpec as P

ATOM_DEV = 16


def padded_2(cells, sides, width):
    for axis, dim in sides:
        count = lax.axis_size(axis)
        head = lax.slice_in_dim(cells, 0, width, axis=dim)
        tail = lax.slice_in_dim(cells, cells.shape[dim] - width, cells.shape[dim], axis=dim)
        cells = jnp.concatenate(
            [
                lax.ppermute(tail, axis, [(i, (i + 1) % count) for i in range(count)]),
                cells,
                lax.ppermute(head, axis, [((i + 1) % count, i) for i in range(count)]),
            ],
            axis=dim,
        )
    return cells


def spline_basis(radii_row, knot_count):
    knot_points = jnp.arange(knot_count).astype(jnp.float32)
    distance = jnp.abs(radii_row[..., None, :] - knot_points[:, None])
    inner_part = 2.0 / 3.0 - distance * distance + 0.5 * distance * distance * distance
    remote = 2.0 - distance
    outer_part = remote * remote * remote / 6.0
    return jnp.where(distance < 1.0, inner_part, jnp.where(distance < 2.0, outer_part, 0.0))


def batch_density(values, row_blocks):
    block_total = values.shape[0]
    band_width = row_blocks.shape[1]
    leading = jnp.zeros((1,) + values.shape[1:], values.dtype)
    trailing = jnp.zeros((band_width - 2,) + values.shape[1:], values.dtype)
    padded = jnp.concatenate([leading, values, trailing], axis=0)
    stacked = jnp.stack(
        [padded[column : column + block_total] for column in range(band_width)], axis=2
    )
    mixed_rows = jnp.einsum(
        "jpkf,jkgf->jpg", stacked, row_blocks, preferred_element_type=jnp.float32
    )
    return jnp.sum(values.astype(jnp.float32) * mixed_rows, axis=(0, 2))


def per_device(
    basis_values,
    density_rows,
    block_mask,
    window_start,
    batch_offsets,
    batch_sizes,
    atom_near,
    harmonics,
    partition,
    radius,
    radial_table,
):
    dev_count = lax.axis_size("dev")
    blocks_dev = density_rows.shape[0]
    block_count = blocks_dev * dev_count
    masked = density_rows * block_mask.astype(jnp.bfloat16)[:, :, None, None]
    first_block = window_start[0]
    positions = jnp.arange(dev_count, dtype=jnp.int32)
    spatial = (first_block + positions) % block_count
    owner_index = spatial % dev_count
    slot_index = spatial // dev_count
    stored = owner_index * blocks_dev + slot_index
    empty_rows = jnp.zeros((dev_count,) + masked.shape[1:], jnp.bfloat16)
    shard_rows = lax.all_gather(masked, "dev", axis=0, tiled=True)
    inside = (stored >= 0) & (stored < shard_rows.shape[0])
    chosen = jnp.take(shard_rows, jnp.clip(stored, 0, shard_rows.shape[0] - 1), axis=0)
    window = jnp.where(inside[:, None, None, None], chosen, empty_rows)

    def one_density(batch_item):
        values, offset = batch_item
        row_blocks = lax.dynamic_slice_in_dim(window, offset, values.shape[0], 0)
        return batch_density(values, row_blocks)

    point_total = basis_values.shape[2]
    alive_mask = (
        jnp.arange(point_total, dtype=jnp.int32)[None, :] < batch_sizes[0][:, None]
    ).astype(jnp.float32)
    density = lax.map(one_density, (basis_values, batch_offsets[0])) * alive_mask
    moment_terms = jnp.einsum(
        "bip,bilp->bil",
        partition * density[:, None, :],
        harmonics.astype(jnp.float32),
        precision=lax.Precision.HIGHEST,
    )
    comp_total = moment_terms.shape[2]
    atom_region = ATOM_DEV * dev_count
    flattened = atom_near.reshape(-1)
    onehot = (flattened[:, None] == jnp.arange(3 * atom_region, dtype=jnp.int32)[None, :]).astype(
        jnp.float32
    )
    partial_value = jnp.dot(
        moment_terms.reshape(-1, comp_total).T, onehot, precision=lax.Precision.HIGHEST
    )
    partial_value = partial_value.reshape(comp_total, 3, atom_region).transpose(1, 0, 2)
    owner_sums = lax.psum_scatter(partial_value, "dev", scatter_dimension=2, tiled=True)
    side_parts = jnp.stack([owner_sums[0], owner_sums[2]])[None]
    rim_parts = padded_2(side_parts, (("region", 0),), 1)
    moments = owner_sums[1] + rim_parts[0, 1] + rim_parts[2, 0]
    own_table = (moments[:, None, :] * radial_table[:, :, None]).astype(jnp.bfloat16)
    rim_table = padded_2(own_table[None], (("region", 0),), 1)
    spline_table = lax.all_gather(rim_table, "dev", axis=3, tiled=True)
    knot_total = radial_table.shape[1]
    batch_total = atom_near.shape[0]
    near_total = atom_near.shape[1]
    table_flat = spline_table.transpose(1, 2, 0, 3).reshape(comp_total, knot_total, 3 * atom_region)
    selected = jnp.take(table_flat, flattened, axis=2).reshape(
        comp_total, knot_total, batch_total, near_total
    )
    spline = spline_basis(radius, knot_total)
    radial = jnp.einsum(
        "lrbi,birp->bilp", selected.astype(jnp.float32), spline, precision=lax.Precision.HIGHEST
    )
    potential = jnp.sum(harmonics.astype(jnp.float32) * radial, axis=(1, 2)) * alive_mask
    return (density, moments, potential)


def solution(mesh):
    placed = (
        P(("region", "dev"), None, None, None),
        P(("region", "dev"), None, None, None),
        P(("region", "dev"), None),
        P(("region", "dev")),
        P(("region", "dev"), None),
        P(("region", "dev"), None),
        P(("region", "dev"), None),
        P(("region", "dev"), None, None, None),
        P(("region", "dev"), None, None),
        P(("region", "dev"), None, None),
        P(),
    )
    return jax.shard_map(
        per_device,
        mesh=mesh,
        in_specs=placed,
        out_specs=(
            P(("region", "dev"), None),
            P(None, ("region", "dev")),
            P(("region", "dev"), None),
        ),
        check_vma=False,
    )
```

profile of v0, /device:TPU:6, one launch (start us, length us, event | category | flops | bytes accessed | tf_op | source)
XLA Modules:
  0.0 498.1 jit_solution(12459849883825730145)
XLA Ops:
  7.2 0.7 convert_element_type.30
  7.9 1.9 broadcast_multiply_fusion
  10.8 127.9 %all-gather.3.cloned.1.call-done = bf16[96,4,128,128]{3,2,1,0:T(8,128)(2,1)} async-done(((bf16[3,4,128,128]{3,2,1,0:T(8,128)(2,1)}), bf16[96,4,128,128]{3,2,1,0:T(8,128)(2,1)}) %all-gather.3.cloned.1.call-update) | async-done | bytes 12582928 | tf_op jit(solution)/shard_map/all_gather | solution.py:73
  138.7 7.6 %gather_fusion = bf16[32,4,128,128]{3,2,1,0:T(8,128)(2,1)} fusion(bf16[96,4,128,128]{3,2,1,0:T(8,128)(2,1)} %all-gather.3.cloned.1.call-done, s32[1024]{0:T(1024)S(1)} %pad_clamp_fusion.1), kind=kCustom, calls=%fused_computation | custom fusion | bytes 8388736 | tf_op jit(solution)/shard_map/jit(_take)/gather | solution.py:75
  146.3 4.7 select_select_fusion
  150.9 63.5 %while.11 = (s32[]{:T(128)}, f32[12,256]{1,0:T(8,128)S(1)}, bf16[12,4,256,128]{3,2,1,0:T(8,128)(2,1)}, s32[12]{0:T(128)S(1)}, bf16[32,4,128,128]{3,2,1,0:T(8,128)(2,1)}) while((s32[]{:T(128)}, f32[12,256]{1,0:T(8,128)S(1)}, bf16[12,4,256,128]{3,2,1,0:T(8,128)(2,1)}, s32[12]{0:T(128)S(1)}, bf16[32,4,128,128]{3,2,1,0:T(8,128)(2,1)}) %tuple.48), condition=%wide.region_2.3_spmd.clone, body=%wide.region_0.2_spmd.sunk.clone | while | flops 136183552 | bytes 3673207 | solution.py:87
  153.5 1.0 dynamic-slice_bitcast_fusion.4
  154.6 1.6 fusion.73
  156.2 0.6 dynamic_slice.23
  158.8 1.0 dynamic-slice_bitcast_fusion.4
  159.9 1.6 fusion.73
  161.5 0.6 dynamic_slice.23
  164.1 1.0 dynamic-slice_bitcast_fusion.4
  165.2 1.6 fusion.73
  166.8 0.6 dynamic_slice.23
  169.4 1.0 dynamic-slice_bitcast_fusion.4
  170.5 1.6 fusion.73
  174.6 1.0 dynamic-slice_bitcast_fusion.4
  175.8 1.6 fusion.73
  179.9 1.0 dynamic-slice_bitcast_fusion.4
  181.1 1.6 fusion.73
  185.2 1.0 dynamic-slice_bitcast_fusion.4
  186.4 1.6 fusion.73
  190.5 1.0 dynamic-slice_bitcast_fusion.4
  191.7 1.6 fusion.73
  195.8 1.0 dynamic-slice_bitcast_fusion.4
  197.0 1.6 fusion.73
  201.1 1.0 dynamic-slice_bitcast_fusion.4
  202.3 1.6 fusion.73
  206.4 1.0 dynamic-slice_bitcast_fusion.4
  207.6 1.6 fusion.73
  211.7 1.0 dynamic-slice_bitcast_fusion.4
  212.8 1.6 fusion.73
  214.6 1.0 fusion.41
  216.0 1.4 copy.37
  217.4 1.3 dynamic-slice
  219.4 156.4 %all-reduce.5.cloned.1.call-done = f32[3,25,512]{1,0,2:T(4,128)} async-done(((f32[3,25,512]{1,0,2:T(4,128)}), f32[3,25,512]{1,0,2:T(4,128)}) %all-reduce.5.cloned.1.call-update) | async-done | bytes 153616
  375.8 0.9 constant_dynamic-slice_fusion.1
  377.2 0.9 collective-permute-done.1
  378.2 4.0 collective-permute-done
  382.3 2.9 collective-permute-start.3
  385.2 1.9 collective-permute-done.2
  387.2 0.7 copy.41
  388.2 90.5 %all-gather.5.cloned.1.call-done = bf16[3,25,16,512]{1,2,0,3:T(8,128)(2,1)} async-done(((bf16[3,25,16,16]{1,2,0,3:T(8,128)(2,1)}), bf16[3,25,16,512]{1,2,0,3:T(8,128)(2,1)}) %all-gather.5.cloned.1.call-update) | async-done | bytes 1228816 | tf_op jit(solution)/shard_map/all_gather | solution.py:110
  478.7 6.5 %copy.51 = bf16[25,16,3,512]{0,1,3,2:T(8,128)(2,1)} copy(bf16[25,16,3,512]{0,1,2,3:T(8,128)(2,1)} %bitcast.76) | data formatting | bytes 2457600 | tf_op jit(solution)/shard_map/reshape | solution.py:114
  485.2 3.4 gather_fusion.1
  488.6 2.2 multiply_reduce_fusion
  490.9 0.7 fusion.44
  (85 shorter events, 8.7 us)
Async XLA Ops:
  7.2 3.3 copy-start.3
  7.2 131.5 %all-gather.3.cloned.1.call-start = ((), (), s32[]{:S(2)}) async-start(), calls=%async_computation | async-start | bytes 12976128 | tf_op jit(solution)/shard_map/all_gather | solution.py:73
  9.8 366.0 %all-reduce.5.cloned.1.call-start = ((), (), s32[]{:S(2)}) async-start(), calls=%async_computation.2 | async-start | bytes 2097152
  146.3 4.7 copy-start.8
  150.9 63.6 %copy-start.5 = (s32[1,12]{1,0:T(1,128)S(1)}, s32[1,12]{1,0:T(1,128)}, u32[]{:S(2)}) copy-start(s32[1,12]{1,0:T(1,128)} %param.18) | copy-start | bytes 148
  150.9 63.6 %copy-start = (f32[12,6,256]{2,1,0:T(8,128)S(1)}, f32[12,6,256]{2,1,0:T(8,128)}, u32[]{:S(2)}) copy-start(f32[12,6,256]{2,1,0:T(8,128)} %param.21) | copy-start | bytes 221188
  150.9 63.7 %copy-start.6 = (bf16[12,6,25,256]{3,2,1,0:T(8,128)(2,1)S(1)}, bf16[12,6,25,256]{3,2,1,0:T(8,128)(2,1)}, u32[]{:S(2)}) copy-start(bf16[12,6,25,256]{3,2,1,0:T(8,128)(2,1)} %param.20) | copy-start | bytes 2764804
  214.6 2.8 copy-start.1
  216.0 166.2 %copy-start.4 = (f32[25,16]{0,1:T(8,128)S(1)}, f32[25,16]{0,1:T(8,128)}, u32[]{:S(2)}) copy-start(f32[25,16]{0,1:T(8,128)} %param.23) | copy-start | bytes 4804
  217.4 261.3 %all-gather.5.cloned.1.call-start = ((), (), s32[]{:S(2)}) async-start(), calls=%async_computation.1 | async-start | bytes 6488064 | tf_op jit(solution)/shard_map/all_gather | solution.py:110
  376.7 1.5 collective-permute-start.1
  376.7 5.5 %collective-permute-start = (f32[1,2,25,16]{2,3,1,0:T(8,128)S(1)}, f32[1,2,25,16]{2,3,1,0:T(8,128)S(1)}, u32[]{:S(2)}, u32[]{:S(2)}) collective-permute-start(f32[1,2,25,16]{2,3,1,0:T(8,128)S(1)} %copy.39), channel_id=1, source_target_pairs={{0,32},{32,64},{64,96},{96,128},{128,160},{160,192},{192,224},{224... | collective-permute-start | bytes 9608 | tf_op jit(solution)/shard_map/ppermute | solution.py:16
  382.2 103.0 %copy-start.2 = (f32[25,16]{0,1:T(8,128)}, f32[25,16]{0,1:T(8,128)S(1)}, u32[]{:S(2)}) copy-start(f32[25,16]{0,1:T(8,128)S(1)} %fusion.47) | copy-start | bytes 4804
  382.2 4.9 collective-permute-start.2
  382.3 4.9 collective-permute-start.3
  478.7 9.9 %copy-start.7 = (f32[12,6,256]{2,1,0:T(8,128)S(1)}, f32[12,6,256]{2,1,0:T(8,128)}, u32[]{:S(2)}) copy-start(f32[12,6,256]{2,1,0:T(8,128)} %param.22) | copy-start | bytes 221188
Sparse Core Ops, SparseCore 0:
  11.2 127.4 all-gather.2
  217.5 158.2 all-reduce.4
  388.1 90.5 all-gather.4
where the time goes:
time: 502 us; the launch traced here: 498 us
  waiting for transfers between devices  382 us (76%)
  local copies, waits for them, and re-layouts  43.2 us (9%)
  loops' own time  23.7 us (5%)
  matrix products  22.3 us (4%)
  between operations  15.2 us (3%)
  other arithmetic  8.15 us (2%)
    unnamed x4, waiting for transfers between devices  156 us
    all_gather x1, waiting for transfers between devices, per_device(): shard_rows = lax.all_gather(masked, 'dev', axis=0, tiled=True)  128 us
    all_gather x1, waiting for transfers between devices, per_device(): spline_table = lax.all_gather(rim_table, 'dev', axis=3, tiled=True)  90.5 us
    another operation x1, loops' own time, per_device(): lax.map(one_density, (basis_values, batch_offsets[0])) * alive_mask  23.7 us
    dot_general x12, matrix products, batch_density(): jnp.einsum('jpkf,jkgf->jpg', stacked, row_blocks, preferred_element_type=...  18.8 us
    another operation x24, local copies, waits for them, and re-layouts, batch_density(): jnp.stack([padded[column:column + block_total] for column in range(band_w...  13.5 us
  transfers between devices with their start and end apart: 7, of which 6 were waited for; matrix products, arithmetic and copies ran while one was open for 0% of the time, Pallas kernels for 0%

commit v1 on v0

v1 whole, which is shorter than its diff:
```python
import functools

import jax
import jax.numpy as jnp
from jax import lax
from jax.experimental import pallas as pl
from jax.experimental.pallas import tpu as pltpu
from jax.sharding import PartitionSpec as P

ATOM_DEV = 16
NX = 4
MESH = pl.DeviceIdType.MESH
NT = (((1,), (1,)), ((), ()))


def place():
    me = lax.axis_index("dev")
    return me % NX, me // NX


def remote(src, dst, send_sem, recv_sem, where):
    return pltpu.make_async_remote_copy(
        src_ref=src,
        dst_ref=dst,
        send_sem=send_sem,
        recv_sem=recv_sem,
        device_id=where,
        device_id_type=MESH,
    )


def greet(peers):
    barrier = pltpu.get_barrier_semaphore()
    for peer in peers:
        pl.semaphore_signal(barrier, inc=1, device_id=peer, device_id_type=MESH)
    pl.semaphore_wait(barrier, len(peers))


def rows_kernel(
    ny,
    rows_ref,
    mask_ref,
    meta_ref,
    win_ref,
    metas_ref,
    own,
    hold,
    out_r,
    out_l,
    out_o,
    out_me,
    relay_l,
    relay_r,
    metas,
    ys,
    yr,
    ms,
    mr,
    rs,
    ls,
    os_,
    fr,
    fl,
    fo,
    frl,
    frr,
    fws,
    local,
):
    x, y = place()
    far = ny // 2
    right = {"dev": y * NX + (x + 1) % NX}
    left = {"dev": y * NX + (x + NX - 1) % NX}
    other = {"dev": y * NX + (x + 2) % NX}
    up = {"dev": ((y + 1) % ny) * NX + x}
    down = {"dev": ((y + ny - 1) % ny) * NX + x}
    slots, band = rows_ref.shape[:2]
    for t in range(slots):
        for k in range(band):
            own[t, k] = rows_ref[t, k] * mask_ref[t * band + k]
    greet((right, left, other, up, down))
    started = []

    def go(copy):
        copy.start()
        started.append(copy)

    go(remote(own, hold.at[0], ys.at[0], yr.at[0], down))
    go(remote(own, hold.at[far], ys.at[far], yr.at[far], up))
    mine = pltpu.make_async_copy(meta_ref, metas.at[0, x], local.at[0])
    mine.start()
    for i, peer in enumerate((right, left, other)):
        go(remote(meta_ref, metas.at[0, x], ms.at[i], mr.at[i], peer))

    def meta_in(i, xx):
        remote(meta_ref, metas.at[0, xx], ms.at[i], mr.at[i], right).wait_recv()

    xr, xl, xo = (x + 1) % NX, (x + NX - 1) % NX, (x + 2) % NX
    meta_in(0, xl)
    meta_in(1, xr)
    meta_in(2, xo)
    mine.wait()
    base = 3
    go(remote(metas.at[0], metas.at[1], ms.at[base], mr.at[base], down))
    go(remote(metas.at[0], metas.at[ny - 1], ms.at[base + far], mr.at[base + far], up))

    order = [0]
    for s in range(1, far + 1):
        order.append(s)
        if s < far:
            order.append(-s)

    def weights(xx, d):
        q = metas[0, xx, 1:2, :]
        m = metas[0, xx, 2:3, :]
        slot = q + jnp.where(m > d, 1, 0)
        slot = jnp.where(slot >= slots, slot - slots, slot)
        return [
            jnp.where(slot == t, 1.0, 0.0).astype(jnp.float32).astype(jnp.bfloat16)
            for t in range(slots)
        ]

    def process(g):
        rho = order[g]
        yy = (y + rho + ny) % ny
        d = yy * NX + x
        source = own if rho == 0 else hold.at[rho - 1 if rho > 0 else far - rho - 1]
        picks = [(xx, dst, weights(xx, d)) for xx, dst in ((xr, out_r), (xl, out_l), (xo, out_o), (x, out_me))]

        def one(k, carry):
            parts = [source[t, k] for t in range(slots)]
            for _, dst, w in picks:
                total = parts[0] * w[0]
                for t in range(1, slots):
                    total = total + parts[t] * w[t]
                dst[g, k] = total
            return carry

        lax.fori_loop(0, band, one, 0)
        go(remote(out_r.at[g], win_ref.at[d], rs.at[g], fl.at[g], right))
        go(remote(out_l.at[g], win_ref.at[d], ls.at[g], fr.at[g], left))
        if g % 2 == 0:
            go(remote(out_o.at[g], relay_l.at[g // 2], os_.at[g], frl.at[g // 2], right))
        else:
            go(remote(out_o.at[g], relay_r.at[g // 2], os_.at[g], frr.at[g // 2], left))
        copy = pltpu.make_async_copy(out_me.at[g], win_ref.at[d], local.at[1 + g])
        copy.start()
        return copy

    def passing(g):
        yy = (y + order[g] + ny) % ny
        i = g // 2
        if g % 2 == 0:
            remote(out_o.at[g], relay_l.at[i], os_.at[g], frl.at[i], right).wait_recv()
            go(remote(relay_l.at[i], win_ref.at[yy * NX + xl], fws.at[g], fo.at[g], right))
        else:
            remote(out_o.at[g], relay_r.at[i], os_.at[g], frr.at[i], left).wait_recv()
            go(remote(relay_r.at[i], win_ref.at[yy * NX + xr], fws.at[g], fo.at[g], left))

    kept = [process(0)]
    done = 0
    for s in range(1, far + 1):
        i = s - 1
        remote(own, hold.at[i], ys.at[i], yr.at[i], down).wait_recv()
        remote(metas.at[0], metas.at[s], ms.at[base + i], mr.at[base + i], down).wait_recv()
        if s < far:
            go(remote(hold.at[i], hold.at[i + 1], ys.at[i + 1], yr.at[i + 1], down))
            go(remote(metas.at[s], metas.at[s + 1], ms.at[base + i + 1], mr.at[base + i + 1], down))
        if s < far:
            j = far + i
            remote(own, hold.at[j], ys.at[j], yr.at[j], up).wait_recv()
            remote(metas.at[0], metas.at[ny - s], ms.at[base + j], mr.at[base + j], up).wait_recv()
            if s < far - 1:
                go(remote(hold.at[j], hold.at[j + 1], ys.at[j + 1], yr.at[j + 1], up))
                go(remote(metas.at[ny - s], metas.at[ny - s - 1], ms.at[base + j + 1], mr.at[base + j + 1], up))
        kept.append(process(2 * s - 1))
        if s < far:
            kept.append(process(2 * s))
        upto = 2 * s - 1
        while done < upto:
            passing(done)
            done += 1
    while done < ny:
        passing(done)
        done += 1
    metas_out = []
    for rho in range(ny):
        copy = pltpu.make_async_copy(metas.at[rho], metas_ref.at[(y + rho) % ny], local.at[1 + ny + rho])
        copy.start()
        metas_out.append(copy)
    for g in range(ny):
        yy = (y + order[g] + ny) % ny
        remote(out_r.at[g], win_ref.at[yy * NX + xl], rs.at[g], fl.at[g], right).wait_recv()
        remote(out_l.at[g], win_ref.at[yy * NX + xr], ls.at[g], fr.at[g], left).wait_recv()
        remote(out_o.at[g], win_ref.at[yy * NX + xo], fws.at[g], fo.at[g], right).wait_recv()
    for copy in started:
        copy.wait_send()
    for copy in kept + metas_out:
        copy.wait()


def gather_rows(rows, mask, meta, ny):
    slots, band, size, _ = rows.shape
    count = ny * NX
    bf, dma = jnp.bfloat16, pltpu.SemaphoreType.DMA
    half = (ny + 1) // 2
    vm = pl.BlockSpec(memory_space=pltpu.VMEM)
    block = (band, size, size)
    return pl.pallas_call(
        functools.partial(rows_kernel, ny),
        name="gather_rows",
        out_shape=(
            jax.ShapeDtypeStruct((count,) + block, bf),
            jax.ShapeDtypeStruct((ny, NX) + meta.shape, jnp.int32),
        ),
        in_specs=[vm, vm, vm],
        out_specs=(pl.BlockSpec(memory_space=pl.ANY), pl.BlockSpec(memory_space=pl.ANY)),
        scratch_shapes=[
            pltpu.VMEM((slots,) + block, bf),
            pltpu.VMEM((ny - 1, slots) + block, bf),
            pltpu.VMEM((ny,) + block, bf),
            pltpu.VMEM((ny,) + block, bf),
            pltpu.VMEM((ny,) + block, bf),
            pltpu.VMEM((ny,) + block, bf),
            pltpu.VMEM((half,) + block, bf),
            pltpu.VMEM((half,) + block, bf),
            pltpu.VMEM((ny, NX) + meta.shape, jnp.int32),
            dma((ny,)),
            dma((ny,)),
            dma((ny + 3,)),
            dma((ny + 3,)),
            dma((ny,)),
            dma((ny,)),
            dma((ny,)),
            dma((ny,)),
            dma((ny,)),
            dma((ny,)),
            dma((half,)),
            dma((half,)),
            dma((ny,)),
            dma((2 * ny + 1,)),
        ],
        compiler_params=pltpu.CompilerParams(collective_id=0, has_side_effects=True),
    )(rows, mask, meta)


def density_kernel(start, offsets, sizes, win_ref, basis_ref, harm_ref, part_ref, dens_ref, terms_ref):
    b = pl.program_id(0)
    count = win_ref.shape[0]
    size = win_ref.shape[2]
    near, comps, points = harm_ref.shape[1:]

    @pl.when(b == 0)
    def _():
        terms_ref[...] = jnp.zeros_like(terms_ref)

    first = start[0] + offsets[b]
    places = [lax.rem(first + j, count) for j in range(4)]

    def piece(j, k):
        return win_ref[places[j], k]

    v = [basis_ref[0, j] for j in range(4)]
    v01 = jnp.concatenate([v[0], v[1]], axis=1)
    v23 = jnp.concatenate([v[2], v[3]], axis=1)

    def quad(a, b_, c, d):
        return jnp.concatenate([jnp.concatenate([a, b_], axis=1), jnp.concatenate([c, d], axis=1)], axis=0)

    zero = jnp.zeros((size, size), jnp.bfloat16)
    dot = functools.partial(lax.dot_general, dimension_numbers=NT, preferred_element_type=jnp.float32)
    m01 = dot(v01, quad(piece(0, 1), piece(0, 2), piece(1, 0), piece(1, 1)))
    m01 = m01 + dot(v23, quad(piece(0, 3), zero, piece(1, 2), piece(1, 3)))
    m23 = dot(v23, quad(piece(2, 1), piece(2, 2), piece(3, 0), piece(3, 1)))
    m2x = dot(v[1], piece(2, 0))
    f32 = jnp.float32
    total = v[0].astype(f32) * m01[:, :size] + v[1].astype(f32) * m01[:, size:]
    total = total + v[2].astype(f32) * (m23[:, :size] + m2x) + v[3].astype(f32) * m23[:, size:]
    row = jnp.sum(total.T, axis=0, keepdims=True)
    lane = lax.broadcasted_iota(jnp.int32, (1, points), 1)
    row = jnp.where(lane < sizes[b], row, 0.0)
    dens_ref[0] = row
    weight = part_ref[0] * row
    spot = lax.broadcasted_iota(jnp.int32, (comps, 128), 1)
    gained = terms_ref[0:comps, :]
    for i in range(near):
        column = jnp.sum(harm_ref[0, i].astype(f32) * weight[i : i + 1, :], axis=1, keepdims=True)
        gained = jnp.where(spot == b * near + i, column, gained)
    terms_ref[0:comps, :] = gained


def densities(start, offsets, sizes, win, basis, harm, part):
    batches, nnb, points, size = basis.shape
    near, comps = harm.shape[1:3]
    return pl.pallas_call(
        density_kernel,
        name="densities",
        out_shape=(
            jax.ShapeDtypeStruct((batches, 1, points), jnp.float32),
            jax.ShapeDtypeStruct((32, 128), jnp.float32),
        ),
        grid_spec=pltpu.PrefetchScalarGridSpec(
            num_scalar_prefetch=3,
            grid=(batches,),
            in_specs=[
                pl.BlockSpec(win.shape, lambda b, *_: (0, 0, 0, 0), pipeline_mode=pl.Buffered(1)),
                pl.BlockSpec((1, nnb, points, size), lambda b, *_: (b, 0, 0, 0)),
                pl.BlockSpec((1, near, comps, points), lambda b, *_: (b, 0, 0, 0)),
                pl.BlockSpec((1, near, points), lambda b, *_: (b, 0, 0)),
            ],
            out_specs=(
                pl.BlockSpec((1, 1, points), lambda b, *_: (b, 0, 0)),
                pl.BlockSpec((32, 128), lambda b, *_: (0, 0)),
            ),
        ),
    )(start, offsets, sizes, win, basis, harm, part)


def moments_kernel(
    ny,
    terms_ref,
    metas_ref,
    out_ref,
    outt_ref,
    every,
    asked,
    hot,
    split,
    answer,
    got,
    ysend,
    yrecv,
    xsend,
    xrecv,
    qsend,
    qrecv,
    zsend,
    zrecv,
    local,
):
    x, y = place()
    region = lax.axis_index("region")
    regions = lax.axis_size("region")
    me = y * NX + x
    ups = [{"dev": ((y + s) % ny) * NX + x} for s in range(1, ny)]
    sides = [{"dev": y * NX + (x + s) % NX} for s in range(1, NX)]
    hops = (1, 2, -1, -2)
    nears = [{"region": (region + h + regions) % regions} for h in hops]
    greet(ups + sides + nears)
    started = []

    def go(copy):
        copy.start()
        started.append(copy)

    for i, s in enumerate(range(1, ny)):
        go(remote(terms_ref, every.at[y, x], ysend.at[i], yrecv.at[i], ups[i]))
    for i in range(len(hops)):
        go(remote(metas_ref.at[y, x], asked.at[i], qsend.at[i], qrecv.at[i], nears[i]))
    mine = pltpu.make_async_copy(terms_ref, every.at[y, x], local.at[0])
    mine.start()
    for i in range(NX - 1):
        go(remote(terms_ref, every.at[y, x], xsend.at[0, i], xrecv.at[0, i], sides[i]))

    def spread(j):
        yy = (y + ny - j) % ny
        remote(terms_ref, every.at[yy, x], ysend.at[j - 1], yrecv.at[j - 1], ups[0]).wait_recv()
        for i in range(NX - 1):
            go(remote(every.at[yy, x], every.at[yy, x], xsend.at[j, i], xrecv.at[j, i], sides[i]))

    near_first = sorted(range(1, ny), key=lambda j: min(j, ny - j))
    count = ny * NX

    def fill(slot, line):
        column = jnp.broadcast_to(line, (128, 128)).T

        def one(t, carry):
            target = metas_ref[t // NX, t % NX, 0:1, :]
            same = jnp.where(column == target, 1.0, 0.0).astype(jnp.float32)
            hot[t, slot * 128 : (slot + 1) * 128, :] = same.astype(jnp.bfloat16)
            return carry

        lax.fori_loop(0, count, one, 0)

    for j in near_first[:2]:
        spread(j)
    fill(0, metas_ref[y, x, 0:1, :])
    for j in near_first[2:4]:
        spread(j)
    for i in range(len(hops)):
        remote(metas_ref.at[y, x], asked.at[i], qsend.at[i], qrecv.at[i], nears[0]).wait_recv()
    fill(1, asked[0, 0:1, :])
    for j in near_first[4:]:
        spread(j)
    for i in range(1, len(hops)):
        fill(1 + i, asked[i, 0:1, :])
    mine.wait()
    for j in range(ny):
        yy = (y + ny - j) % ny
        for i in range(NX - 1):
            xx = (x + NX - 1 - i) % NX
            remote(terms_ref, every.at[yy, xx], xsend.at[j, i], xrecv.at[j, i], sides[0]).wait_recv()

    def parts(t, carry):
        value = every[t // NX, t % NX]
        high = value.astype(jnp.bfloat16)
        split[t, 0:32, :] = high
        split[t, 32:64, :] = (value - high.astype(jnp.float32)).astype(jnp.bfloat16)
        return carry

    lax.fori_loop(0, count, parts, 0)

    def add(t, total):
        left = jnp.concatenate([split[2 * t], split[2 * t + 1]], axis=1)
        right = jnp.concatenate([hot[2 * t], hot[2 * t + 1]], axis=1)
        return total + lax.dot_general(left, right, NT, preferred_element_type=jnp.float32)

    width = 128 * (1 + len(hops))
    sums = lax.fori_loop(0, count // 2, add, jnp.zeros((64, width), jnp.float32))
    sums = sums[0:32, :] + sums[32:64, :]
    for i in range(len(hops)):
        answer[i] = sums[:, 128 * (i + 1) : 128 * (i + 2)]
    for i in range(len(hops)):
        back = {"region": (region - hops[i] + regions) % regions}
        go(remote(answer.at[i], got.at[i], zsend.at[i], zrecv.at[i], back))
    whole = sums[:, 0:128]
    for i in range(len(hops)):
        remote(answer.at[i], got.at[i], zsend.at[i], zrecv.at[i], nears[0]).wait_recv()
        whole = whole + got[i]
    out_ref[...] = whole
    outt_ref[...] = jnp.concatenate([whole, jnp.zeros((96, 128), jnp.float32)], axis=0).T
    for copy in started:
        copy.wait_send()


def sum_moments(terms, metas, ny):
    count = ny * NX
    dma = pltpu.SemaphoreType.DMA
    vm = pl.BlockSpec(memory_space=pltpu.VMEM)
    f32, bf = jnp.float32, jnp.bfloat16
    return pl.pallas_call(
        functools.partial(moments_kernel, ny),
        name="sum_moments",
        out_shape=(jax.ShapeDtypeStruct((32, 128), f32), jax.ShapeDtypeStruct((128, 128), f32)),
        in_specs=[vm, vm],
        out_specs=(vm, vm),
        scratch_shapes=[
            pltpu.VMEM((ny, NX, 32, 128), f32),
            pltpu.VMEM((4,) + metas.shape[2:], jnp.int32),
            pltpu.VMEM((count, 640, 128), bf),
            pltpu.VMEM((count, 64, 128), bf),
            pltpu.VMEM((4, 32, 128), f32),
            pltpu.VMEM((4, 32, 128), f32),
            dma((ny - 1,)),
            dma((ny - 1,)),
            dma((ny, NX - 1)),
            dma((ny, NX - 1)),
            dma((4,)),
            dma((4,)),
            dma((4,)),
            dma((4,)),
            dma((1,)),
        ],
        compiler_params=pltpu.CompilerParams(collective_id=1, has_side_effects=True),
    )(terms, metas)


def potential_kernel(sizes, moments_ref, radial_ref, harm_ref, radius_ref, pot_ref):
    b = pl.program_id(0)
    near, comps, points = harm_ref.shape[1:]
    knots = radial_ref.shape[0]
    f32 = jnp.float32
    knot = lax.broadcasted_iota(jnp.int32, (knots, points), 0).astype(f32)
    total = jnp.zeros((knots, points), f32)
    for i in range(near):
        moment = moments_ref[pl.ds(b * near + i, 1), 0:comps]
        table = (moment * radial_ref[...]).astype(jnp.bfloat16)
        mixed = jnp.dot(table, harm_ref[0, i], preferred_element_type=f32)
        distance = jnp.abs(radius_ref[0, i : i + 1, :] - knot)
        inner = 2.0 / 3.0 - distance * distance + 0.5 * distance * distance * distance
        remote_ = 2.0 - distance
        outer = remote_ * remote_ * remote_ * (1.0 / 6.0)
        spline = jnp.where(distance < 1.0, inner, jnp.where(distance < 2.0, outer, 0.0))
        total = total + mixed * spline
    row = jnp.sum(total, axis=0, keepdims=True)
    lane = lax.broadcasted_iota(jnp.int32, (1, points), 1)
    pot_ref[0] = jnp.where(lane < sizes[b], row, 0.0)


def potentials(sizes, moments, radial, harm, radius):
    batches, near, comps, points = harm.shape
    return pl.pallas_call(
        potential_kernel,
        name="potentials",
        out_shape=jax.ShapeDtypeStruct((batches, 1, points), jnp.float32),
        grid_spec=pltpu.PrefetchScalarGridSpec(
            num_scalar_prefetch=1,
            grid=(batches,),
            in_specs=[
                pl.BlockSpec(moments.shape, lambda b, *_: (0, 0)),
                pl.BlockSpec(radial.shape, lambda b, *_: (0, 0)),
                pl.BlockSpec((1, near, comps, points), lambda b, *_: (b, 0, 0, 0)),
                pl.BlockSpec((1, near, points), lambda b, *_: (b, 0, 0)),
            ],
            out_specs=pl.BlockSpec((1, 1, points), lambda b, *_: (b, 0, 0)),
        ),
    )(sizes, moments, radial, harm, radius)


def per_device(
    basis_values,
    density_rows,
    block_mask,
    window_start,
    batch_offsets,
    batch_sizes,
    atom_near,
    harmonics,
    partition,
    radius,
    radial_table,
):
    devs = lax.axis_size("dev")
    regions = lax.axis_size("region")
    ny = devs // NX
    me, region = lax.axis_index("dev"), lax.axis_index("region")
    atom_region = ATOM_DEV * devs
    batches, near = atom_near.shape
    pairs = batches * near
    comps = radial_table.shape[0]
    flat = atom_near.reshape(pairs)
    target = lax.rem(region + flat // atom_region - 1 + regions, regions) * atom_region + flat % atom_region
    owned = region * atom_region + me * ATOM_DEV + jnp.arange(ATOM_DEV, dtype=jnp.int32)
    line = jnp.concatenate([target, owned, jnp.full((128 - pairs - ATOM_DEV,), -1, jnp.int32)])
    start = window_start[0]
    meta = jnp.stack(
        [
            line,
            jnp.full((128,), start // devs, jnp.int32),
            jnp.full((128,), start % devs, jnp.int32),
            jnp.zeros((128,), jnp.int32),
        ]
    )
    mask = jnp.broadcast_to(block_mask.reshape(-1)[:, None, None], (block_mask.size, 1, 128)).astype(jnp.bfloat16)
    win, metas = gather_rows(density_rows, mask, meta, ny)
    density, terms = densities(
        window_start, batch_offsets[0], batch_sizes[0], win, basis_values, harmonics, partition
    )
    sums, sums_t = sum_moments(terms, metas, ny)
    moments = sums[:comps, pairs : pairs + ATOM_DEV]
    potential = potentials(batch_sizes[0], sums_t, radial_table.T, harmonics, radius)
    points = basis_values.shape[2]
    return (density.reshape(batches, points), moments, potential.reshape(batches, points))


def solution(mesh):
    placed = (
        P(("region", "dev"), None, None, None),
        P(("region", "dev"), None, None, None),
        P(("region", "dev"), None),
        P(("region", "dev")),
        P(("region", "dev"), None),
        P(("region", "dev"), None),
        P(("region", "dev"), None),
        P(("region", "dev"), None, None, None),
        P(("region", "dev"), None, None),
        P(("region", "dev"), None, None),
        P(),
    )
    return jax.shard_map(
        per_device,
        mesh=mesh,
        in_specs=placed,
        out_specs=(
            P(("region", "dev"), None),
            P(None, ("region", "dev")),
            P(("region", "dev"), None),
        ),
        check_vma=False,
    )
```

time: 502 us -> 124 us (0.25)
  waiting for transfers between devices: 382 us -> 0 us
  Pallas kernels: 0 us -> 114 us
  local copies, waits for them, and re-layouts: 43.2 us -> 4.65 us
  loops' own time: 23.7 us -> 0 us
  matrix products: 22.3 us -> 0 us
  between operations: 15.2 us -> 1.35 us
  other arithmetic: 8.15 us -> 1.44 us
    all_gather x2 -> x0, waiting for transfers between devices: 218 us -> none  [the longest x1 128 us: per_device(): shard_rows = lax.all_gather(masked, 'dev', axis=0, tiled=True)]
    unnamed x4 -> x0, waiting for transfers between devices: 156 us -> none
    pallas_call x0 -> x4, Pallas kernels: none -> 114 us  [the longest x1 62.4 us: gather_rows(): pl.pallas_call(functools.partial(rows_kernel, ny), name='gather_rows', ou...]
    another operation x1 -> x0, loops' own time: 23.7 us -> none  [per_device(): lax.map(one_density, (basis_values, batch_offsets[0])) * alive_mask]
    dot_general x15 -> x0, matrix products: 22.3 us -> none  [the longest x12 18.8 us: batch_density(): jnp.einsum('jpkf,jkgf->jpg', stacked, row_blocks, preferred_element_type=...]
    another operation x24 -> x3, local copies, waits for them, and re-layouts: 13.5 us -> 0.22 us  [per_device(): jnp.stack([line, jnp.full((128,), start // devs, jnp.int32), jnp.full((12...]
    gather x2 -> x0, local copies, waits for them, and re-layouts: 11 us -> none  [the longest x1 7.58 us: per_device(): jnp.take(shard_rows, jnp.clip(stored, 0, shard_rows.shape[0] - 1), axis=0)]
    dynamic_slice x12 -> x0, local copies, waits for them, and re-layouts: 7.04 us -> none  [per_device(): lax.map(one_density, (basis_values, batch_offsets[0])) * alive_mask]
  transfers between devices with their start and end apart: 7 -> 0, of which waited for: 6 -> 0; matrix products, arithmetic and copies ran while one was open for 0% -> 0% of each run, Pallas kernels for 0% -> 0%
where the time goes in v1:
time: 124 us; the launch traced here: 121 us
  Pallas kernels  114 us (92%)
  local copies, waits for them, and re-layouts  4.65 us (4%)
  other arithmetic  1.44 us (1%)
  between operations  1.35 us (1%)
    pallas_call x1, Pallas kernels, gather_rows(): pl.pallas_call(functools.partial(rows_kernel, ny), name='gather_rows', ou...  62.4 us
    pallas_call x1, Pallas kernels, sum_moments(): pl.pallas_call(functools.partial(moments_kernel, ny), name='sum_moments',...  30.9 us
    pallas_call x1, Pallas kernels, densities(): pl.pallas_call(density_kernel, name='densities', out_shape=(jax.ShapeDtyp...  12.6 us
    pallas_call x1, Pallas kernels, potentials(): pl.pallas_call(potential_kernel, name='potentials', out_shape=jax.ShapeDt...  8.27 us
    unnamed x3, local copies, waits for them, and re-layouts  2.79 us

profile of v1, /device:TPU:6, one launch (start us, length us, event | category | flops | bytes accessed | tf_op | source)
XLA Modules:
  0.0 121.5 jit_solution(1853861400634274724)
XLA Ops:
  1.3 0.1 pad.1.clone
  1.4 0.1 pad.2.clone
  1.5 0.1 pad.3.clone
  1.5 0.7 convert_element_type.5
  2.2 0.1 convert_element_type.6
  2.3 0.7 broadcast_in_dim.8.mask_ref
  3.0 0.8 copy.16
  3.8 0.1 reshape.25
  3.9 0.1 add_bitcast_fusion
  4.0 0.7 add_add_fusion.meta_ref
  4.6 62.4 %gather_rows.1 = (bf16[32,4,128,128]{3,2,1,0:T(8,128)(2,1)}, s32[8,4,4,128]{3,2,1,0:T(4,128)}) custom-call(bf16[3,4,128,128]{3,2,1,0:T(8,128)(2,1)} %rows_ref.1, bf16[12,1,128]{2,1,0:T(2,128)(2,1)} %broadcast_in_dim.8.mask_ref, s32[4,128]{1,0:T(4,128)} %add_add_fusion.meta_ref), custom_call_target="tpu_custom_call" | custom-call | tf_op jit(solution)/shard_map/gather_rows/pallas_call | solution.py:209
  67.0 12.6 %densities.1 = (f32[12,1,256]{2,1,0:T(1,128)}, f32[32,128]{1,0:T(8,128)}) custom-call(s32[1]{0:T(128)} %copy.22.start, s32[12]{0:T(128)} %bitcast.20, s32[12]{0:T(128)} %bitcast.18, bf16[32,4,128,128]{3,2,1,0:T(8,128)(2,1)} %get-tuple-element.9.win_ref, bf16[12,4,256,128]{3,2,1,0:T(8,128)(2,1)} %basis_ref.1, bf16[12,6,25,256]{3,2,1,0:T(8,128)(2,1)} %harm_ref.3, ...), custom_call_target="tpu_custom_call" | custom-call | tf_op jit(solution)/shard_map/densities/pallas_call | solution.py:295
  79.5 30.9 %sum_moments.1 = (f32[32,128]{1,0:T(8,128)}, f32[128,128]{1,0:T(8,128)}) custom-call(f32[32,128]{1,0:T(8,128)} %get-tuple-element.11.terms_ref, s32[8,4,4,128]{3,2,1,0:T(4,128)} %get-tuple-element.12.metas_ref), custom_call_target="tpu_custom_call" | custom-call | tf_op jit(solution)/shard_map/sum_moments/pallas_call | solution.py:441
  110.4 0.8 slice.3
  111.2 0.7 copy.17
  111.9 8.3 %potentials.1 = f32[12,1,256]{2,1,0:T(1,128)} custom-call(s32[12]{0:T(128)} %bitcast.19, f32[128,128]{1,0:T(8,128)} %get-tuple-element.14.moments_ref, f32[16,25]{1,0:T(8,128)} %bitcast.17, bf16[12,6,25,256]{3,2,1,0:T(8,128)(2,1)} %harm_ref.3, f32[12,6,256]{2,1,0:T(8,128)} %radius_ref.1), custom_call_target="tpu_custom_call" | custom-call | tf_op jit(solution)/shard_map/potentials/pallas_call | solution.py:492
  120.1 1.3 %copy_bitcast_fusion = (f32[12,256]{1,0:T(8,128)}, f32[12,256]{1,0:T(8,128)}) fusion(f32[12,1,256]{2,1,0:T(1,128)} %potentials.1, f32[12,1,256]{2,1,0:T(1,128)} %get-tuple-element.10), kind=kLoop, calls=%fused_computation | loop fusion | bytes 49152
  (3 shorter events, 0.0 us)

commit v2 on v0

v2 whole, which is shorter than its diff:
```python
import functools

import jax
import jax.numpy as jnp
from jax import lax
from jax.experimental import pallas as pl
from jax.experimental.pallas import tpu as pltpu
from jax.sharding import PartitionSpec as P

ATOM_DEV = 16
NX = 4
CHUNKS = 4
HOPS = (1, 2, -1, -2)
MESH = pl.DeviceIdType.MESH
NT = (((1,), (1,)), ((), ()))
TN = (((0,), (0,)), ((), ()))
F32, BF = jnp.float32, jnp.bfloat16


def remote(src, dst, send_sem, recv_sem, where):
    return pltpu.make_async_remote_copy(
        src_ref=src,
        dst_ref=dst,
        send_sem=send_sem,
        recv_sem=recv_sem,
        device_id=where,
        device_id_type=MESH,
    )


def spline_values(radii, knots):
    knot = lax.broadcasted_iota(jnp.int32, (knots, radii.shape[1]), 0).astype(F32)
    distance = jnp.abs(radii - knot)
    inner = 2.0 / 3.0 - distance * distance + 0.5 * distance * distance * distance
    rest = 2.0 - distance
    outer = rest * rest * rest * (1.0 / 6.0)
    return jnp.where(distance < 1.0, inner, jnp.where(distance < 2.0, outer, 0.0))


def pack(terms, pairs):
    lane = lax.broadcasted_iota(jnp.int32, (8, 128), 1)
    row = lax.broadcasted_iota(jnp.int32, (8, 128), 0)
    third = terms[16:24]
    last = jnp.broadcast_to(terms[24:25], (8, 128))
    top = jnp.where(lane < pairs, terms[0:8], pltpu.roll(third, 72, 1))
    tail = jnp.where(row == 0, pltpu.roll(last, 88, 1), jnp.where(row == 1, pltpu.roll(last, 48, 1), 0.0))
    low = jnp.where(lane < pairs, terms[8:16], jnp.where(lane < 88, pltpu.roll(third, 16, 1), tail))
    return top, low


def unpack(top, low, pairs):
    lane = lax.broadcasted_iota(jnp.int32, (8, 128), 1)
    row = lax.broadcasted_iota(jnp.int32, (8, 128), 0)
    live = lane < pairs
    first = jnp.where(live, top, 0.0)
    second = jnp.where(live, low, 0.0)
    third = jnp.where(lane < 56, pltpu.roll(top, 56, 1), jnp.where(live, pltpu.roll(low, 112, 1), 0.0))
    zero = jnp.broadcast_to(low[0:1], (8, 128))
    one = jnp.broadcast_to(low[1:2], (8, 128))
    last = jnp.where(lane < 40, pltpu.roll(zero, 40, 1), jnp.where(live, pltpu.roll(one, 80, 1), 0.0))
    last = jnp.where(row == 0, last, 0.0)
    return jnp.concatenate([first, second, third, last], axis=0)


def kernel(
    ny,
    rows_ref,
    mask_ref,
    start_ref,
    offsets_ref,
    sizes_ref,
    near_ref,
    part_ref,
    radius_ref,
    radial_ref,
    basis_hbm,
    harm_hbm,
    dens_ref,
    mom_ref,
    pot_ref,
    own,
    hold,
    out_r,
    out_l,
    out_o,
    relay,
    win,
    line,
    metas,
    asked,
    basis,
    harm,
    turned,
    parted,
    radial,
    packed,
    every,
    hot,
    sums,
    answer,
    got,
    ys,
    yr,
    ms,
    mr,
    qs,
    qr,
    rs,
    ls,
    os_,
    fr,
    fl,
    fo,
    frel,
    fws,
    ts,
    tr,
    xs,
    xr_,
    zs,
    zr,
    local,
):
    region, me = lax.axis_index("region"), lax.axis_index("dev")
    regions, devs = lax.axis_size("region"), ny * NX
    x, y = me % NX, me // NX
    far = ny // 2
    xr, xl, xo = (x + 1) % NX, (x + NX - 1) % NX, (x + 2) % NX
    right, left, other = ({"dev": y * NX + xx} for xx in (xr, xl, xo))
    ups = [{"dev": ((y + s) % ny) * NX + x} for s in range(1, ny)]
    up, down = ups[0], ups[-1]
    nears = [{"region": (region + h + regions) % regions} for h in HOPS]
    slots, band, size, _ = rows_ref.shape
    step = band // CHUNKS
    near, batches = near_ref.shape
    pairs = near * batches
    knots, comps = radial_ref.shape
    points = part_ref.shape[2]
    started = []

    def go(copy):
        copy.start()
        started.append(copy)

    barrier = pltpu.get_barrier_semaphore()
    greeted = ups + [right, left, other] + nears
    for peer in greeted:
        pl.semaphore_signal(barrier, inc=1, device_id=peer, device_id_type=MESH)
    fetch_basis = pltpu.make_async_copy(basis_hbm, basis, local.at[0])
    fetch_basis.start()
    fetch_harm = pltpu.make_async_copy(harm_hbm, harm, local.at[1])
    fetch_harm.start()

    for t in range(slots):
        for k in range(band):
            keep = jnp.full((1, 1), mask_ref[t, k], jnp.int32).astype(F32).astype(BF)
            own[k, t] = rows_ref[t, k] * keep

    lane = lax.broadcasted_iota(jnp.int32, (1, 128), 1)
    line[...] = jnp.zeros_like(line)
    line[0:near, 0:batches] = near_ref[...]
    total = jnp.zeros((1, 128), jnp.int32)
    for i in range(near):
        moved = pltpu.roll(jnp.broadcast_to(line[i : i + 1, :], (8, 128)), i * batches, 1)[0:1]
        total = jnp.where((lane >= i * batches) & (lane < (i + 1) * batches), moved, total)
    atom_region = ATOM_DEV * devs
    bits = atom_region.bit_length() - 1
    side = region + lax.shift_right_logical(total, bits) - 1
    side = jnp.where(side < 0, side + regions, jnp.where(side >= regions, side - regions, side))
    target = side * atom_region + (total & (atom_region - 1))
    owned = region * atom_region + me * ATOM_DEV + lane - pairs
    whole_line = jnp.where(lane < pairs, target, jnp.where(lane < pairs + ATOM_DEV, owned, -1))
    start = start_ref[0]
    line[0:1] = whole_line
    line[1:2] = jnp.full((1, 128), start // devs, jnp.int32)
    line[2:3] = jnp.full((1, 128), start % devs, jnp.int32)
    metas[0, x] = line[0:4]
    pl.semaphore_wait(barrier, len(greeted))

    def part_of(ref, c):
        return ref.at[pl.ds(c * step, step)]

    for c in range(CHUNKS):
        go(remote(part_of(own, c), part_of(hold.at[0], c), ys.at[0, c], yr.at[0, c], down))
        go(remote(part_of(own, c), part_of(hold.at[far], c), ys.at[far, c], yr.at[far, c], up))
        if c == 0:
            for i, peer in enumerate((right, left, other)):
                go(remote(line.at[0:4], metas.at[0, x], ms.at[i], mr.at[i], peer))
    for i in range(len(HOPS)):
        go(remote(line.at[0:4], asked.at[i], qs.at[i], qr.at[i], nears[i]))

    for i, xx in enumerate((xl, xr, xo)):
        remote(line.at[0:4], metas.at[0, xx], ms.at[i], mr.at[i], right).wait_recv()
    base = 3
    go(remote(metas.at[0], metas.at[1], ms.at[base], mr.at[base], down))
    go(remote(metas.at[0], metas.at[ny - 1], ms.at[base + far], mr.at[base + far], up))

    order = [0]
    for s in range(1, far + 1):
        order.append(s)
        if s < far:
            order.append(-s)

    def row_of(g):
        return (y + order[g] + ny) % ny

    def weights(xx, d):
        q = metas[0, xx, 1:2, :]
        m = metas[0, xx, 2:3, :]
        slot = q + jnp.where(m > d, 1, 0)
        slot = jnp.where(slot >= slots, slot - slots, slot)
        return [jnp.where(slot == t, 1.0, 0.0).astype(F32).astype(BF) for t in range(slots)]

    def via_right(g, c):
        return (g + c) % 2 == 0

    def process(g, c):
        rho = order[g]
        d = row_of(g) * NX + x
        source = own if rho == 0 else hold.at[rho - 1 if rho > 0 else far - rho - 1]
        picks = [(dst, weights(xx, d)) for xx, dst in ((xr, out_r.at[g]), (xl, out_l.at[g]), (xo, out_o.at[g]), (x, win.at[d]))]
        for k in range(c * step, (c + 1) * step):
            parts = [source[k, t] for t in range(slots)]
            for dst, w in picks:
                chosen = parts[0] * w[0]
                for t in range(1, slots):
                    chosen = chosen + parts[t] * w[t]
                dst[k] = chosen
        go(remote(part_of(out_o.at[g], c), part_of(relay.at[g], c), os_.at[g, c], frel.at[g, c], right if via_right(g, c) else left))
        go(remote(part_of(out_r.at[g], c), part_of(win.at[d], c), rs.at[g, c], fl.at[g, c], right))
        go(remote(part_of(out_l.at[g], c), part_of(win.at[d], c), ls.at[g, c], fr.at[g, c], left))

    def passing(g, c):
        toward, origin = (right, xl) if via_right(g, c) else (left, xr)
        d = row_of(g) * NX + origin
        remote(part_of(out_o.at[g], c), part_of(relay.at[g], c), os_.at[g, c], frel.at[g, c], right).wait_recv()
        go(remote(part_of(relay.at[g], c), part_of(win.at[d], c), fws.at[g, c], fo.at[g, c], toward))

    def prepare(b, carry):
        for j in range(band):
            turned[b, j * size : (j + 1) * size, :] = basis[b, j].T
        for i in range(near):
            values = harm[b, i].astype(F32)
            parted[b, i] = values * part_ref[b, i : i + 1, :]
            spline = spline_values(radius_ref[b, i : i + 1, :], knots)
            curve = lax.dot_general(
                radial_ref[...], spline, TN, precision=lax.Precision.HIGHEST, preferred_element_type=F32
            )
            radial[b, i] = values * curve
        return carry

    def fill(slot, asked_line):
        column = jnp.broadcast_to(asked_line, (128, 128)).T

        def one(t, carry):
            r = lax.rem(t // NX + ny - y, ny)
            wanted = metas[r, t % NX, 0:1, :]
            same = jnp.where(column == wanted, 1.0, 0.0).astype(F32)
            hot[t, slot * 128 : (slot + 1) * 128, :] = same.astype(BF)
            return carry

        lax.fori_loop(0, devs, one, 0)

    for c in range(CHUNKS):
        process(0, c)
    fetch_basis.wait()
    fetch_harm.wait()
    per = -(-batches // (CHUNKS * (far - 1)))
    ready = 0
    lag = []
    for s in range(1, far + 1):
        i, j = s - 1, far + s - 1
        for c in range(CHUNKS):
            remote(part_of(own, c), part_of(hold.at[i], c), ys.at[i, c], yr.at[i, c], down).wait_recv()
            if s < far:
                go(remote(part_of(hold.at[i], c), part_of(hold.at[i + 1], c), ys.at[i + 1, c], yr.at[i + 1, c], down))
                remote(part_of(own, c), part_of(hold.at[j], c), ys.at[j, c], yr.at[j, c], up).wait_recv()
                if s < far - 1:
                    go(remote(part_of(hold.at[j], c), part_of(hold.at[j + 1], c), ys.at[j + 1, c], yr.at[j + 1, c], up))
            if c == 0:
                remote(metas.at[0], metas.at[s], ms.at[base + i], mr.at[base + i], down).wait_recv()
                if s < far:
                    go(remote(metas.at[s], metas.at[s + 1], ms.at[base + i + 1], mr.at[base + i + 1], down))
                    remote(metas.at[0], metas.at[ny - s], ms.at[base + j], mr.at[base + j], up).wait_recv()
                    if s < far - 1:
                        go(remote(metas.at[ny - s], metas.at[ny - s - 1], ms.at[base + j + 1], mr.at[base + j + 1], up))
            process(2 * s - 1, c)
            if s < far:
                process(2 * s, c)
            if s == 1:
                lag.append((0, c))
            else:
                lag.append((2 * s - 3, c))
                lag.append((2 * s - 2, c))
            while lag:
                passing(*lag.pop(0))
            if ready < batches and s < far:
                upto = min(batches, ready + per)
                lax.fori_loop(ready, upto, prepare, 0)
                ready = upto
    for i in range(len(HOPS)):
        remote(line.at[0:4], asked.at[i], qs.at[i], qr.at[i], nears[0]).wait_recv()
    fill(0, metas[0, x, 0:1, :])
    fill(1, asked[0, 0:1, :])
    for c in range(CHUNKS):
        passing(ny - 1, c)
    for i in range(1, len(HOPS)):
        fill(1 + i, asked[i, 0:1, :])
    for g in range(ny):
        row = row_of(g) * NX
        for c in range(CHUNKS):
            remote(part_of(out_r.at[g], c), part_of(win.at[row + xl], c), rs.at[g, c], fl.at[g, c], right).wait_recv()
            remote(part_of(out_l.at[g], c), part_of(win.at[row + xr], c), ls.at[g, c], fr.at[g, c], left).wait_recv()
            remote(part_of(out_o.at[g], c), part_of(win.at[row + xo], c), fws.at[g, c], fo.at[g, c], right).wait_recv()

    zero = jnp.zeros((size, size), BF)
    wide = lax.broadcasted_iota(jnp.int32, (1, points), 1)
    spot = lax.broadcasted_iota(jnp.int32, (comps, 128), 1)

    def batch(b, gained):
        first = start + offsets_ref[0, b]
        places = [lax.rem(first + j, devs) for j in range(band)]

        def piece(j, k):
            return win[places[j], k]

        def quad(a, b_, c, d):
            return jnp.concatenate([jnp.concatenate([a, b_], axis=1), jnp.concatenate([c, d], axis=1)], axis=0)

        low, high = turned[b, 0 : 2 * size, :], turned[b, 2 * size : 4 * size, :]
        dot = functools.partial(jnp.dot, preferred_element_type=F32)
        m01 = dot(quad(piece(0, 1), piece(0, 2), piece(1, 0), piece(1, 1)), low)
        m01 = m01 + dot(quad(piece(0, 3), zero, piece(1, 2), piece(1, 3)), high)
        m23 = dot(quad(piece(2, 1), piece(2, 2), piece(3, 0), piece(3, 1)), high)
        m2x = dot(piece(2, 0), turned[b, size : 2 * size, :])
        density = jnp.sum(m01 * low.astype(F32) + m23 * high.astype(F32), axis=0, keepdims=True)
        density = density + jnp.sum(m2x * turned[b, 2 * size : 3 * size, :].astype(F32), axis=0, keepdims=True)
        density = jnp.where(wide < sizes_ref[0, b], density, 0.0)
        dens_ref[b] = density
        for i in range(near):
            column = jnp.sum(parted[b, i] * density, axis=1, keepdims=True)
            gained = jnp.where(spot == i * batches + b, column, gained)
        return gained

    terms = lax.fori_loop(0, batches, batch, jnp.zeros((comps, 128), F32))
    top, low = pack(terms, pairs)
    packed[0:8] = top
    packed[8:16] = low

    sides = [{"dev": y * NX + (x + s) % NX} for s in range(1, NX)]
    for i in range(ny - 1):
        go(remote(packed, every.at[y, x], ts.at[i], tr.at[i], ups[i]))
    for i in range(NX - 1):
        go(remote(packed, every.at[y, x], xs.at[0, i], xr_.at[0, i], sides[i]))
    every[y, x] = packed[...]
    near_first = sorted(range(1, ny), key=lambda j: min(j, ny - j))

    def spread(j):
        yy = (y + ny - j) % ny
        remote(packed, every.at[yy, x], ts.at[j - 1], tr.at[j - 1], up).wait_recv()
        for i in range(NX - 1):
            go(remote(every.at[yy, x], every.at[yy, x], xs.at[j, i], xr_.at[j, i], sides[i]))

    sums[...] = jnp.zeros_like(sums)

    def collect(j):
        yy = (y + ny - j) % ny
        for i in range(NX - 1):
            xx = (x + NX - 1 - i) % NX
            remote(packed, every.at[yy, xx], xs.at[j, i], xr_.at[j, i], right).wait_recv()
        for pair in range(NX // 2):
            lefts, rights = [], []
            for xx in (2 * pair, 2 * pair + 1):
                value = unpack(every[yy, xx, 0:8], every[yy, xx, 8:16], pairs)
                high = value.astype(BF)
                lowp = (value - high.astype(F32)).astype(BF)
                lefts.append(jnp.concatenate([high, lowp], axis=0))
                rights.append(hot[yy * NX + xx])
            sums[...] += lax.dot_general(
                jnp.concatenate(lefts, axis=1), jnp.concatenate(rights, axis=1), NT, preferred_element_type=F32
            )

    for j in near_first:
        spread(j)
    collect(0)
    for j in near_first:
        collect(j)
    both = sums[0:32, :] + sums[32:64, :]
    for i in range(len(HOPS)):
        answer[i] = both[:, 128 * (i + 1) : 128 * (i + 2)]
    for i in range(len(HOPS)):
        back = {"region": (region - HOPS[i] + regions) % regions}
        go(remote(answer.at[i], got.at[i], zs.at[i], zr.at[i], back))
    moment = both[:, 0:128]
    for i in range(len(HOPS)):
        remote(answer.at[i], got.at[i], zs.at[i], zr.at[i], nears[0]).wait_recv()
        moment = moment + got[i]
    upright = jnp.concatenate([moment, jnp.zeros((96, 128), F32)], axis=0).T
    mom_ref[...] = upright[pairs : pairs + ATOM_DEV, 0:comps]
    for b in range(batches):
        gathered = jnp.zeros((comps, points), F32)
        for i in range(near):
            q = i * batches + b
            gathered = gathered + radial[b, i] * moment[0:comps, q : q + 1]
        value = jnp.sum(gathered, axis=0, keepdims=True)
        pot_ref[b] = jnp.where(wide < sizes_ref[0, b], value, 0.0)
    for copy in started:
        copy.wait_send()


def per_device(
    basis_values,
    density_rows,
    block_mask,
    window_start,
    batch_offsets,
    batch_sizes,
    atom_near,
    harmonics,
    partition,
    radius,
    radial_table,
):
    devs = lax.axis_size("dev")
    ny = devs // NX
    slots, band, size, _ = density_rows.shape
    batches, near = atom_near.shape
    comps, knots = radial_table.shape
    points = basis_values.shape[2]
    dma = pltpu.SemaphoreType.DMA
    vm = pl.BlockSpec(memory_space=pltpu.VMEM)
    sm = pl.BlockSpec(memory_space=pltpu.SMEM)
    hb = pl.BlockSpec(memory_space=pl.ANY)
    block = (band, size, size)
    kept = (band, slots, size, size)
    hops = len(HOPS)
    density, moments, potential = pl.pallas_call(
        functools.partial(kernel, ny),
        name="whole_step",
        out_shape=(
            jax.ShapeDtypeStruct((batches, 1, points), F32),
            jax.ShapeDtypeStruct((ATOM_DEV, comps), F32),
            jax.ShapeDtypeStruct((batches, 1, points), F32),
        ),
        in_specs=[vm, sm, sm, sm, sm, vm, vm, vm, vm, hb, hb],
        out_specs=(vm, vm, vm),
        scratch_shapes=[
            pltpu.VMEM(kept, BF),
            pltpu.VMEM((ny - 1,) + kept, BF),
            pltpu.VMEM((ny,) + block, BF),
            pltpu.VMEM((ny,) + block, BF),
            pltpu.VMEM((ny,) + block, BF),
            pltpu.VMEM((ny,) + block, BF),
            pltpu.VMEM((devs,) + block, BF),
            pltpu.VMEM((8, 128), jnp.int32),
            pltpu.VMEM((ny, NX, 4, 128), jnp.int32),
            pltpu.VMEM((hops, 4, 128), jnp.int32),
            pltpu.VMEM(basis_values.shape, BF),
            pltpu.VMEM(harmonics.shape, BF),
            pltpu.VMEM((batches, band * size, points), BF),
            pltpu.VMEM((batches, near, comps, points), F32),
            pltpu.VMEM((batches, near, comps, points), F32),
            pltpu.VMEM((16, 128), F32),
            pltpu.VMEM((ny, NX, 16, 128), F32),
            pltpu.VMEM((devs, 128 * (1 + hops), 128), BF),
            pltpu.VMEM((64, 128 * (1 + hops)), F32),
            pltpu.VMEM((hops, 32, 128), F32),
            pltpu.VMEM((hops, 32, 128), F32),
            dma((ny - 1, CHUNKS)),
            dma((ny - 1, CHUNKS)),
            dma((ny + 3,)),
            dma((ny + 3,)),
            dma((hops,)),
            dma((hops,)),
            dma((ny, CHUNKS)),
            dma((ny, CHUNKS)),
            dma((ny, CHUNKS)),
            dma((ny, CHUNKS)),
            dma((ny, CHUNKS)),
            dma((ny, CHUNKS)),
            dma((ny, CHUNKS)),
            dma((ny, CHUNKS)),
            dma((ny - 1,)),
            dma((ny - 1,)),
            dma((ny, NX - 1)),
            dma((ny, NX - 1)),
            dma((hops,)),
            dma((hops,)),
            dma((2,)),
        ],
        compiler_params=pltpu.CompilerParams(collective_id=0, has_side_effects=True),
    )(
        density_rows,
        block_mask,
        window_start,
        batch_offsets,
        batch_sizes,
        atom_near.T,
        partition,
        radius,
        radial_table.T,
        basis_values,
        harmonics,
    )
    return density.reshape(batches, points), moments.T, potential.reshape(batches, points)


def solution(mesh):
    placed = (
        P(("region", "dev"), None, None, None),
        P(("region", "dev"), None, None, None),
        P(("region", "dev"), None),
        P(("region", "dev")),
        P(("region", "dev"), None),
        P(("region", "dev"), None),
        P(("region", "dev"), None),
        P(("region", "dev"), None, None, None),
        P(("region", "dev"), None, None),
        P(("region", "dev"), None, None),
        P(),
    )
    return jax.shard_map(
        per_device,
        mesh=mesh,
        in_specs=placed,
        out_specs=(
            P(("region", "dev"), None),
            P(None, ("region", "dev")),
            P(("region", "dev"), None),
        ),
        check_vma=False,
    )
```

time: 502 us -> 96.2 us (0.19)
  waiting for transfers between devices: 382 us -> 0 us
  Pallas kernels: 0 us -> 91.9 us
  local copies, waits for them, and re-layouts: 43.2 us -> 2.63 us
  loops' own time: 23.7 us -> 0 us
  matrix products: 22.3 us -> 0 us
  between operations: 15.2 us -> 1.29 us
  other arithmetic: 8.15 us -> 0 us
    all_gather x2 -> x0, waiting for transfers between devices: 218 us -> none  [the longest x1 128 us: per_device(): shard_rows = lax.all_gather(masked, 'dev', axis=0, tiled=True)]
    unnamed x4 -> x0, waiting for transfers between devices: 156 us -> none
    pallas_call x0 -> x1, Pallas kernels: none -> 91.9 us  [per_device(): pl.pallas_call(functools.partial(kernel, ny), name='whole_step', out_shap...]
    another operation x1 -> x0, loops' own time: 23.7 us -> none  [per_device(): lax.map(one_density, (basis_values, batch_offsets[0])) * alive_mask]
    dot_general x15 -> x0, matrix products: 22.3 us -> none  [the longest x12 18.8 us: batch_density(): jnp.einsum('jpkf,jkgf->jpg', stacked, row_blocks, preferred_element_type=...]
    another operation x24 -> x0, local copies, waits for them, and re-layouts: 13.5 us -> none  [batch_density(): jnp.stack([padded[column:column + block_total] for column in range(band_w...]
    gather x2 -> x0, local copies, waits for them, and re-layouts: 11 us -> none  [the longest x1 7.58 us: per_device(): jnp.take(shard_rows, jnp.clip(stored, 0, shard_rows.shape[0] - 1), axis=0)]
    dynamic_slice x12 -> x0, local copies, waits for them, and re-layouts: 7.04 us -> none  [per_device(): lax.map(one_density, (basis_values, batch_offsets[0])) * alive_mask]
  transfers between devices with their start and end apart: 7 -> 0, of which waited for: 6 -> 0; matrix products, arithmetic and copies ran while one was open for 0% -> 0% of each run, Pallas kernels for 0% -> 0%
where the time goes in v2:
time: 96.2 us; the launch traced here: 95.8 us
  Pallas kernels  91.9 us (96%)
  local copies, waits for them, and re-layouts  2.63 us (3%)
  between operations  1.29 us (1%)
    pallas_call x1, Pallas kernels, per_device(): pl.pallas_call(functools.partial(kernel, ny), name='whole_step', out_shap...  91.9 us
    unnamed x2, local copies, waits for them, and re-layouts  2.63 us

profile of v2, /device:TPU:6, one launch (start us, length us, event | category | flops | bytes accessed | tf_op | source)
XLA Modules:
  0.0 95.8 jit_solution(2377720123617503634)
XLA Ops:
  1.3 91.9 %whole_step.1 = (f32[12,1,256]{2,1,0:T(1,128)}, f32[16,25]{1,0:T(8,128)}, f32[12,1,256]{2,1,0:T(1,128)}) custom-call(bf16[3,4,128,128]{3,2,1,0:T(8,128)(2,1)} %rows_ref.1, s32[3,4]{1,0:T(4,128)} %mask_ref.1, s32[1]{0:T(128)S(6)} %copy.19.start_ref, s32[1,12]{1,0:T(1,128)} %offsets_ref.1, s32[1,12]{1,0:T(1,128)} %sizes_ref.1, s32[6,12]{1,0:T(8,128)} %bitcast.9, ...), custom_call_target="tpu_custom_call" | custom-call | tf_op jit(solution)/shard_map/whole_step/pallas_call | solution.py:437
  93.2 1.3 %copy_bitcast_fusion = (f32[12,256]{1,0:T(8,128)}, f32[12,256]{1,0:T(8,128)}) fusion(f32[12,1,256]{2,1,0:T(1,128)} %get-tuple-element.8, f32[12,1,256]{2,1,0:T(1,128)} %get-tuple-element.6), kind=kLoop, calls=%fused_computation | loop fusion | bytes 49152
  94.5 1.3 %copy.20 = f32[25,16]{0,1:T(8,128)} copy(f32[25,16]{0,1:T(8,128)} %bitcast.8) | data formatting | bytes 3200

commit v3 on v2

--- a/solution.py
+++ b/solution.py
@@ -9,7 +9,7 @@
 
 ATOM_DEV = 16
 NX = 4
-CHUNKS = 4
+CHUNKS = 2
 HOPS = (1, 2, -1, -2)
 MESH = pl.DeviceIdType.MESH
 NT = (((1,), (1,)), ((), ()))
@@ -84,6 +84,8 @@
     out_l,
     out_o,
     relay,
+    swap,
+    across,
     win,
     line,
     metas,
@@ -113,6 +115,10 @@
     fo,
     frel,
     fws,
+    sws,
+    swr,
+    acs,
+    acr,
     ts,
     tr,
     xs,
@@ -191,6 +197,10 @@
 
     for i, xx in enumerate((xl, xr, xo)):
         remote(line.at[0:4], metas.at[0, xx], ms.at[i], mr.at[i], right).wait_recv()
+    lone, halfway = band - 1, size // 2
+    first_half, second_half = pl.ds(0, halfway), pl.ds(halfway, halfway)
+    go(remote(own.at[lone, :, first_half], swap.at[0], sws.at[0], swr.at[0], right))
+    go(remote(own.at[lone, :, second_half], swap.at[1], sws.at[1], swr.at[1], left))
     base = 3
     go(remote(metas.at[0], metas.at[1], ms.at[base], mr.at[base], down))
     go(remote(metas.at[0], metas.at[ny - 1], ms.at[base + far], mr.at[base + far], up))
@@ -210,6 +220,10 @@
         slot = q + jnp.where(m > d, 1, 0)
         slot = jnp.where(slot >= slots, slot - slots, slot)
         return [jnp.where(slot == t, 1.0, 0.0).astype(F32).astype(BF) for t in range(slots)]
+
+    def other_part(c):
+        low, high = c * step, min((c + 1) * step, lone)
+        return pl.ds(low, high - low) if high > low else None
 
     def via_right(g, c):
         return (g + c) % 2 == 0
@@ -221,20 +235,49 @@
         picks = [(dst, weights(xx, d)) for xx, dst in ((xr, out_r.at[g]), (xl, out_l.at[g]), (xo, out_o.at[g]), (x, win.at[d]))]
         for k in range(c * step, (c + 1) * step):
             parts = [source[k, t] for t in range(slots)]
-            for dst, w in picks:
+            for n, (dst, w) in enumerate(picks):
+                if n == 2 and k == lone:
+                    continue
                 chosen = parts[0] * w[0]
                 for t in range(1, slots):
                     chosen = chosen + parts[t] * w[t]
                 dst[k] = chosen
-        go(remote(part_of(out_o.at[g], c), part_of(relay.at[g], c), os_.at[g, c], frel.at[g, c], right if via_right(g, c) else left))
+        if other_part(c) is not None:
+            some = other_part(c)
+            go(remote(out_o.at[g, some], relay.at[g, some], os_.at[g, c], frel.at[g, c], right if via_right(g, c) else left))
         go(remote(part_of(out_r.at[g], c), part_of(win.at[d], c), rs.at[g, c], fl.at[g, c], right))
         go(remote(part_of(out_l.at[g], c), part_of(win.at[d], c), ls.at[g, c], fr.at[g, c], left))
 
     def passing(g, c):
+        some = other_part(c)
+        if some is None:
+            return
         toward, origin = (right, xl) if via_right(g, c) else (left, xr)
         d = row_of(g) * NX + origin
-        remote(part_of(out_o.at[g], c), part_of(relay.at[g], c), os_.at[g, c], frel.at[g, c], right).wait_recv()
-        go(remote(part_of(relay.at[g], c), part_of(win.at[d], c), fws.at[g, c], fo.at[g, c], toward))
+        remote(out_o.at[g, some], relay.at[g, some], os_.at[g, c], frel.at[g, c], right).wait_recv()
+        go(remote(relay.at[g, some], win.at[d, some], fws.at[g, c], fo.at[g, c], toward))
+
+    def take(g):
+        rho = order[g]
+        d = row_of(g) * NX + xo
+        source = across.at[0 if rho == 0 else (rho if rho > 0 else far - rho)]
+        w = weights(x, d)
+        chosen = source[0] * w[0]
+        for t in range(1, slots):
+            chosen = chosen + source[t] * w[t]
+        win[d, lone] = chosen
+
+    def across_in(s):
+        i, j = s - 1, far + s - 1
+        remote(across.at[0], across.at[1 + i], acs.at[i], acr.at[i], down).wait_recv()
+        if s < far:
+            go(remote(across.at[1 + i], across.at[2 + i], acs.at[i + 1], acr.at[i + 1], down))
+            remote(across.at[0], across.at[1 + j], acs.at[j], acr.at[j], up).wait_recv()
+            if s < far - 1:
+                go(remote(across.at[1 + j], across.at[2 + j], acs.at[j + 1], acr.at[j + 1], up))
+        take(2 * s - 1)
+        if s < far:
+            take(2 * s)
 
     def prepare(b, carry):
         for j in range(band):
@@ -263,6 +306,10 @@
 
     for c in range(CHUNKS):
         process(0, c)
+    remote(own.at[lone, :, first_half], swap.at[0], sws.at[0], swr.at[0], right).wait_recv()
+    go(remote(swap.at[0], across.at[0, :, first_half], sws.at[2], swr.at[2], right))
+    remote(own.at[lone, :, second_half], swap.at[1], sws.at[1], swr.at[1], left).wait_recv()
+    go(remote(swap.at[1], across.at[0, :, second_half], sws.at[3], swr.at[3], left))
     fetch_basis.wait()
     fetch_harm.wait()
     per = -(-batches // (CHUNKS * (far - 1)))
@@ -272,11 +319,14 @@
         i, j = s - 1, far + s - 1
         for c in range(CHUNKS):
             remote(part_of(own, c), part_of(hold.at[i], c), ys.at[i, c], yr.at[i, c], down).wait_recv()
+            if s < far - 1 or (s < far and c % 2 == 0):
+                go(remote(part_of(hold.at[i], c), part_of(hold.at[i + 1], c), ys.at[i + 1, c], yr.at[i + 1, c], down))
             if s < far:
-                go(remote(part_of(hold.at[i], c), part_of(hold.at[i + 1], c), ys.at[i + 1, c], yr.at[i + 1, c], down))
                 remote(part_of(own, c), part_of(hold.at[j], c), ys.at[j, c], yr.at[j, c], up).wait_recv()
                 if s < far - 1:
                     go(remote(part_of(hold.at[j], c), part_of(hold.at[j + 1], c), ys.at[j + 1, c], yr.at[j + 1, c], up))
+                elif c % 2 == 1:
+                    go(remote(part_of(hold.at[j], c), part_of(hold.at[far - 1], c), ys.at[far - 1, c], yr.at[far - 1, c], up))
             if c == 0:
                 remote(metas.at[0], metas.at[s], ms.at[base + i], mr.at[base + i], down).wait_recv()
                 if s < far:
@@ -298,6 +348,14 @@
                 upto = min(batches, ready + per)
                 lax.fori_loop(ready, upto, prepare, 0)
                 ready = upto
+        if s == 1:
+            remote(swap.at[0], across.at[0, :, first_half], sws.at[2], swr.at[2], right).wait_recv()
+            remote(swap.at[1], across.at[0, :, second_half], sws.at[3], swr.at[3], left).wait_recv()
+            go(remote(across.at[0], across.at[1], acs.at[0], acr.at[0], down))
+            go(remote(across.at[0], across.at[1 + far], acs.at[far], acr.at[far], up))
+            take(0)
+        else:
+            across_in(s - 1)
     for i in range(len(HOPS)):
         remote(line.at[0:4], asked.at[i], qs.at[i], qr.at[i], nears[0]).wait_recv()
     fill(0, metas[0, x, 0:1, :])
@@ -306,12 +364,15 @@
         passing(ny - 1, c)
     for i in range(1, len(HOPS)):
         fill(1 + i, asked[i, 0:1, :])
+    across_in(far)
     for g in range(ny):
         row = row_of(g) * NX
         for c in range(CHUNKS):
             remote(part_of(out_r.at[g], c), part_of(win.at[row + xl], c), rs.at[g, c], fl.at[g, c], right).wait_recv()
             remote(part_of(out_l.at[g], c), part_of(win.at[row + xr], c), ls.at[g, c], fr.at[g, c], left).wait_recv()
-            remote(part_of(out_o.at[g], c), part_of(win.at[row + xo], c), fws.at[g, c], fo.at[g, c], right).wait_recv()
+            some = other_part(c)
+            if some is not None:
+                remote(out_o.at[g, some], win.at[row + xo, some], fws.at[g, c], fo.at[g, c], right).wait_recv()
 
     zero = jnp.zeros((size, size), BF)
     wide = lax.broadcasted_iota(jnp.int32, (1, points), 1)
@@ -336,13 +397,13 @@
         density = jnp.sum(m01 * low.astype(F32) + m23 * high.astype(F32), axis=0, keepdims=True)
         density = density + jnp.sum(m2x * turned[b, 2 * size : 3 * size, :].astype(F32), axis=0, keepdims=True)
         density = jnp.where(wide < sizes_ref[0, b], density, 0.0)
-        dens_ref[b] = density
+        dens_ref[pl.ds(b, 1), :] = density
         for i in range(near):
             column = jnp.sum(parted[b, i] * density, axis=1, keepdims=True)
             gained = jnp.where(spot == i * batches + b, column, gained)
         return gained
 
-    terms = lax.fori_loop(0, batches, batch, jnp.zeros((comps, 128), F32))
+    terms = lax.fori_loop(0, batches, batch, jnp.zeros((comps, 128), F32), unroll=4)
     top, low = pack(terms, pairs)
     packed[0:8] = top
     packed[8:16] = low
@@ -403,9 +464,24 @@
             q = i * batches + b
             gathered = gathered + radial[b, i] * moment[0:comps, q : q + 1]
         value = jnp.sum(gathered, axis=0, keepdims=True)
-        pot_ref[b] = jnp.where(wide < sizes_ref[0, b], value, 0.0)
+        pot_ref[b : b + 1, :] = jnp.where(wide < sizes_ref[0, b], value, 0.0)
     for copy in started:
         copy.wait_send()
+
+
+def hand_over(*arrays):
+    def copies(*refs):
+        for source, target in zip(refs[: len(arrays)], refs[len(arrays) :]):
+            target[...] = source[...]
+
+    vm = pl.BlockSpec(memory_space=pltpu.VMEM)
+    return pl.pallas_call(
+        copies,
+        name="hand_over",
+        out_shape=tuple(jax.ShapeDtypeStruct(a.shape, a.dtype) for a in arrays),
+        in_specs=[vm] * len(arrays),
+        out_specs=(vm,) * len(arrays),
+    )(*arrays)
 
 
 def per_device(
@@ -438,9 +514,9 @@
         functools.partial(kernel, ny),
         name="whole_step",
         out_shape=(
-            jax.ShapeDtypeStruct((batches, 1, points), F32),
+            jax.ShapeDtypeStruct((batches, points), F32),
             jax.ShapeDtypeStruct((ATOM_DEV, comps), F32),
-            jax.ShapeDtypeStruct((batches, 1, points), F32),
+            jax.ShapeDtypeStruct((batches, points), F32),
         ),
         in_specs=[vm, sm, sm, sm, sm, vm, vm, vm, vm, hb, hb],
         out_specs=(vm, vm, vm),
@@ -451,6 +527,8 @@
             pltpu.VMEM((ny,) + block, BF),
             pltpu.VMEM((ny,) + block, BF),
             pltpu.VMEM((ny,) + block, BF),
+            pltpu.VMEM((2, slots, size // 2, size), BF),
+            pltpu.VMEM((ny, slots, size, size), BF),
             pltpu.VMEM((devs,) + block, BF),
             pltpu.VMEM((8, 128), jnp.int32),
             pltpu.VMEM((ny, NX, 4, 128), jnp.int32),
@@ -480,6 +558,10 @@
             dma((ny, CHUNKS)),
             dma((ny, CHUNKS)),
             dma((ny, CHUNKS)),
+            dma((4,)),
+            dma((4,)),
+            dma((ny - 1,)),
+            dma((ny - 1,)),
             dma((ny - 1,)),
             dma((ny - 1,)),
             dma((ny, NX - 1)),
@@ -502,7 +584,8 @@
         basis_values,
         harmonics,
     )
-    return density.reshape(batches, points), moments.T, potential.reshape(batches, points)
+    density, moments, potential = hand_over(density, moments, potential)
+    return density, moments.T, potential
 
 
 def solution(mesh):

time: 96.2 us -> 85.3 us (0.89)
  Pallas kernels: 91.9 us -> 83.8 us
  local copies, waits for them, and re-layouts: 2.63 us -> 0 us
    pallas_call x1, Pallas kernels: 91.9 us -> 82.4 us  [per_device(): pl.pallas_call(functools.partial(kernel, ny), name='whole_step', out_shap...]
    unnamed x2 -> x0, local copies, waits for them, and re-layouts: 2.63 us -> none
    pallas_call x0 -> x1, Pallas kernels: none -> 1.37 us  [hand_over(): pl.pallas_call(copies, name='hand_over', out_shape=tuple((jax.ShapeDtypeS...]
where the time goes in v3:
time: 85.3 us; the launch traced here: 85.1 us
  Pallas kernels  83.8 us (98%)
  between operations  1.29 us (2%)
    pallas_call x1, Pallas kernels, per_device(): pl.pallas_call(functools.partial(kernel, ny), name='whole_step', out_shap...  82.4 us

profile of v3, /device:TPU:6, one launch (start us, length us, event | category | flops | bytes accessed | tf_op | source)
XLA Modules:
  0.0 85.1 jit_solution(6209105798727867129)
XLA Ops:
  1.3 82.4 %whole_step.1 = (f32[12,256]{1,0:T(8,128)}, f32[16,25]{1,0:T(8,128)}, f32[12,256]{1,0:T(8,128)}) custom-call(bf16[3,4,128,128]{3,2,1,0:T(8,128)(2,1)} %rows_ref.1, s32[3,4]{1,0:T(4,128)} %mask_ref.1, s32[1]{0:T(128)S(6)} %copy.14.start_ref, s32[1,12]{1,0:T(1,128)} %offsets_ref.1, s32[1,12]{1,0:T(1,128)} %sizes_ref.1, s32[6,12]{1,0:T(8,128)} %bitcast.4, ...), custom_call_target="tpu_custom_call" | custom-call | tf_op jit(solution)/shard_map/whole_step/pallas_call | solution.py:513
  83.7 1.4 %hand_over.1 = (f32[12,256]{1,0:T(8,128)}, f32[16,25]{1,0:T(8,128)}, f32[12,256]{1,0:T(8,128)}) custom-call(f32[12,256]{1,0:T(8,128)} %get-tuple-element.9.refs_0_, f32[16,25]{1,0:T(8,128)} %get-tuple-element.10.refs_1_, f32[12,256]{1,0:T(8,128)} %get-tuple-element.11.refs_2_), custom_call_target="tpu_custom_call" | custom-call | tf_op jit(solution)/shard_map/hand_over/pallas_call | solution.py:478

commit v4 on v3

--- a/solution.py
+++ b/solution.py
@@ -64,20 +64,23 @@
 
 def kernel(
     ny,
-    rows_ref,
+    rows_hbm,
     mask_ref,
     start_ref,
     offsets_ref,
     sizes_ref,
     near_ref,
-    part_ref,
-    radius_ref,
+    part_hbm,
+    radius_hbm,
     radial_ref,
     basis_hbm,
     harm_hbm,
     dens_ref,
     mom_ref,
     pot_ref,
+    rows_ref,
+    part_ref,
+    radius_ref,
     own,
     hold,
     out_r,
@@ -149,18 +152,20 @@
         started.append(copy)
 
     barrier = pltpu.get_barrier_semaphore()
-    greeted = ups + [right, left, other] + nears
+    greeted = [up, down, right, left, other] + nears
     for peer in greeted:
         pl.semaphore_signal(barrier, inc=1, device_id=peer, device_id_type=MESH)
-    fetch_basis = pltpu.make_async_copy(basis_hbm, basis, local.at[0])
-    fetch_basis.start()
-    fetch_harm = pltpu.make_async_copy(harm_hbm, harm, local.at[1])
-    fetch_harm.start()
-
-    for t in range(slots):
-        for k in range(band):
-            keep = jnp.full((1, 1), mask_ref[t, k], jnp.int32).astype(F32).astype(BF)
-            own[k, t] = rows_ref[t, k] * keep
+    fetch_rows = pltpu.make_async_copy(rows_hbm, rows_ref, local.at[2])
+    fetch_rows.start()
+    fetches = [
+        pltpu.make_async_copy(source, target, local.at[n])
+        for source, target, n in (
+            (basis_hbm, basis, 0),
+            (harm_hbm, harm, 1),
+            (part_hbm, part_ref, 3),
+            (radius_hbm, radius_ref, 4),
+        )
+    ]
 
     lane = lax.broadcasted_iota(jnp.int32, (1, 128), 1)
     line[...] = jnp.zeros_like(line)
@@ -181,6 +186,11 @@
     line[1:2] = jnp.full((1, 128), start // devs, jnp.int32)
     line[2:3] = jnp.full((1, 128), start % devs, jnp.int32)
     metas[0, x] = line[0:4]
+    fetch_rows.wait()
+    for t in range(slots):
+        for k in range(band):
+            keep = jnp.full((1, 1), mask_ref[t, k], jnp.int32).astype(F32).astype(BF)
+            own[k, t] = rows_ref[t, k] * keep
     pl.semaphore_wait(barrier, len(greeted))
 
     def part_of(ref, c):
@@ -195,15 +205,19 @@
     for i in range(len(HOPS)):
         go(remote(line.at[0:4], asked.at[i], qs.at[i], qr.at[i], nears[i]))
 
-    for i, xx in enumerate((xl, xr, xo)):
-        remote(line.at[0:4], metas.at[0, xx], ms.at[i], mr.at[i], right).wait_recv()
+    for copy in fetches:
+        copy.start()
+
+    def row_meta(i):
+        remote(line.at[0:4], metas.at[0, (xl, xr, xo)[i]], ms.at[i], mr.at[i], right).wait_recv()
+
+    row_meta(0)
+    row_meta(1)
     lone, halfway = band - 1, size // 2
     first_half, second_half = pl.ds(0, halfway), pl.ds(halfway, halfway)
     go(remote(own.at[lone, :, first_half], swap.at[0], sws.at[0], swr.at[0], right))
     go(remote(own.at[lone, :, second_half], swap.at[1], sws.at[1], swr.at[1], left))
     base = 3
-    go(remote(metas.at[0], metas.at[1], ms.at[base], mr.at[base], down))
-    go(remote(metas.at[0], metas.at[ny - 1], ms.at[base + far], mr.at[base + far], up))
 
     order = [0]
     for s in range(1, far + 1):
@@ -225,32 +239,41 @@
         low, high = c * step, min((c + 1) * step, lone)
         return pl.ds(low, high - low) if high > low else None
 
+    def straight(g, c):
+        return g == ny - 1 and c == CHUNKS - 1
+
     def via_right(g, c):
         return (g + c) % 2 == 0
 
-    def process(g, c):
+    def process(g, c, some=(0, 1, 2, 3)):
         rho = order[g]
         d = row_of(g) * NX + x
         source = own if rho == 0 else hold.at[rho - 1 if rho > 0 else far - rho - 1]
-        picks = [(dst, weights(xx, d)) for xx, dst in ((xr, out_r.at[g]), (xl, out_l.at[g]), (xo, out_o.at[g]), (x, win.at[d]))]
+        picks = ((xr, out_r.at[g]), (xl, out_l.at[g]), (xo, out_o.at[g]), (x, win.at[d]))
+        picks = [(n, (picks[n][1], weights(picks[n][0], d))) for n in some]
         for k in range(c * step, (c + 1) * step):
             parts = [source[k, t] for t in range(slots)]
-            for n, (dst, w) in enumerate(picks):
+            for n, (dst, w) in picks:
                 if n == 2 and k == lone:
                     continue
                 chosen = parts[0] * w[0]
                 for t in range(1, slots):
                     chosen = chosen + parts[t] * w[t]
                 dst[k] = chosen
-        if other_part(c) is not None:
-            some = other_part(c)
-            go(remote(out_o.at[g, some], relay.at[g, some], os_.at[g, c], frel.at[g, c], right if via_right(g, c) else left))
+        if 2 in some and other_part(c) is not None:
+            piece = other_part(c)
+            if straight(g, c):
+                go(remote(out_o.at[g, piece], win.at[d, piece], os_.at[g, c], fo.at[g, c], other))
+            else:
+                go(remote(out_o.at[g, piece], relay.at[g, piece], os_.at[g, c], frel.at[g, c], right if via_right(g, c) else left))
+        if 0 not in some:
+            return
         go(remote(part_of(out_r.at[g], c), part_of(win.at[d], c), rs.at[g, c], fl.at[g, c], right))
         go(remote(part_of(out_l.at[g], c), part_of(win.at[d], c), ls.at[g, c], fr.at[g, c], left))
 
     def passing(g, c):
         some = other_part(c)
-        if some is None:
+        if some is None or straight(g, c):
             return
         toward, origin = (right, xl) if via_right(g, c) else (left, xr)
         d = row_of(g) * NX + origin
@@ -305,13 +328,18 @@
         lax.fori_loop(0, devs, one, 0)
 
     for c in range(CHUNKS):
-        process(0, c)
+        process(0, c, (0, 1))
+    row_meta(2)
+    go(remote(metas.at[0], metas.at[1], ms.at[base], mr.at[base], down))
+    go(remote(metas.at[0], metas.at[ny - 1], ms.at[base + far], mr.at[base + far], up))
+    for c in range(CHUNKS):
+        process(0, c, (2, 3))
     remote(own.at[lone, :, first_half], swap.at[0], sws.at[0], swr.at[0], right).wait_recv()
     go(remote(swap.at[0], across.at[0, :, first_half], sws.at[2], swr.at[2], right))
     remote(own.at[lone, :, second_half], swap.at[1], sws.at[1], swr.at[1], left).wait_recv()
     go(remote(swap.at[1], across.at[0, :, second_half], sws.at[3], swr.at[3], left))
-    fetch_basis.wait()
-    fetch_harm.wait()
+    for copy in fetches:
+        copy.wait()
     per = -(-batches // (CHUNKS * (far - 1)))
     ready = 0
     lag = []
@@ -518,9 +546,12 @@
             jax.ShapeDtypeStruct((ATOM_DEV, comps), F32),
             jax.ShapeDtypeStruct((batches, points), F32),
         ),
-        in_specs=[vm, sm, sm, sm, sm, vm, vm, vm, vm, hb, hb],
+        in_specs=[hb, sm, sm, sm, sm, vm, hb, hb, vm, hb, hb],
         out_specs=(vm, vm, vm),
         scratch_shapes=[
+            pltpu.VMEM(density_rows.shape, BF),
+            pltpu.VMEM(partition.shape, F32),
+            pltpu.VMEM(radius.shape, F32),
             pltpu.VMEM(kept, BF),
             pltpu.VMEM((ny - 1,) + kept, BF),
             pltpu.VMEM((ny,) + block, BF),
@@ -568,7 +599,7 @@
             dma((ny, NX - 1)),
             dma((hops,)),
             dma((hops,)),
-            dma((2,)),
+            dma((5,)),
         ],
         compiler_params=pltpu.CompilerParams(collective_id=0, has_side_effects=True),
     )(

time: 85.3 us -> 83.4 us (0.978)
  Pallas kernels: 83.8 us -> 81.2 us
    pallas_call x1, Pallas kernels: 82.4 us -> 79.9 us  [per_device(): pl.pallas_call(functools.partial(kernel, ny), name='whole_step', out_shap...]
where the time goes in v4:
time: 83.4 us; the launch traced here: 82.5 us
  Pallas kernels  81.2 us (97%)
  between operations  1.29 us (2%)
    pallas_call x1, Pallas kernels, per_device(): pl.pallas_call(functools.partial(kernel, ny), name='whole_step', out_shap...  79.9 us

profile of v4, /device:TPU:6, one launch (start us, length us, event | category | flops | bytes accessed | tf_op | source)
XLA Modules:
  0.0 82.5 jit_solution(7030519368258853229)
XLA Ops:
  1.3 79.9 %whole_step.1 = (f32[12,256]{1,0:T(8,128)}, f32[16,25]{1,0:T(8,128)}, f32[12,256]{1,0:T(8,128)}) custom-call(bf16[3,4,128,128]{3,2,1,0:T(8,128)(2,1)} %rows_hbm.1, s32[3,4]{1,0:T(4,128)} %mask_ref.1, s32[1]{0:T(128)S(6)} %copy.14.start_ref, s32[1,12]{1,0:T(1,128)} %offsets_ref.1, s32[1,12]{1,0:T(1,128)} %sizes_ref.1, s32[6,12]{1,0:T(8,128)} %bitcast.4, ...), custom_call_target="tpu_custom_call" | custom-call | tf_op jit(solution)/shard_map/whole_step/pallas_call | solution.py:541
  81.1 1.4 %hand_over.1 = (f32[12,256]{1,0:T(8,128)}, f32[16,25]{1,0:T(8,128)}, f32[12,256]{1,0:T(8,128)}) custom-call(f32[12,256]{1,0:T(8,128)} %get-tuple-element.9.refs_0_, f32[16,25]{1,0:T(8,128)} %get-tuple-element.10.refs_1_, f32[12,256]{1,0:T(8,128)} %get-tuple-element.11.refs_2_), custom_call_target="tpu_custom_call" | custom-call | tf_op jit(solution)/shard_map/hand_over/pallas_call | solution.py:506

commit v5 on v4

--- a/solution.py
+++ b/solution.py
@@ -60,6 +60,24 @@
     last = jnp.where(lane < 40, pltpu.roll(zero, 40, 1), jnp.where(live, pltpu.roll(one, 80, 1), 0.0))
     last = jnp.where(row == 0, last, 0.0)
     return jnp.concatenate([first, second, third, last], axis=0)
+
+
+def pack_sums(sums):
+    lane = lax.broadcasted_iota(jnp.int32, (8, 128), 1)
+    row = lax.broadcasted_iota(jnp.int32, (8, 128), 0)
+    last = jnp.broadcast_to(sums[24:25], (8, 128))
+    tail = jnp.where(row == 1, pltpu.roll(last, 48, 1), jnp.where(row == 2, pltpu.roll(last, 8, 1), 0.0))
+    tail = jnp.where(row == 0, pltpu.roll(last, 88, 1), tail)
+    return jnp.concatenate([jnp.where(lane < 88, sums[0:8], tail), sums[8:24]], axis=0)
+
+
+def unpack_sums(packed):
+    lane = lax.broadcasted_iota(jnp.int32, (8, 128), 1)
+    row = lax.broadcasted_iota(jnp.int32, (8, 128), 0)
+    lines = [jnp.broadcast_to(packed[n : n + 1], (8, 128)) for n in range(3)]
+    last = jnp.where(lane < 80, pltpu.roll(lines[1], 80, 1), pltpu.roll(lines[2], 120, 1))
+    last = jnp.where(lane < 40, pltpu.roll(lines[0], 40, 1), last)
+    return jnp.concatenate([packed, jnp.where((row == 0) & (lane < 88), last, 0.0)], axis=0)
 
 
 def kernel(
@@ -124,8 +142,6 @@
     acr,
     ts,
     tr,
-    xs,
-    xr_,
     zs,
     zr,
     local,
@@ -202,8 +218,6 @@
         if c == 0:
             for i, peer in enumerate((right, left, other)):
                 go(remote(line.at[0:4], metas.at[0, x], ms.at[i], mr.at[i], peer))
-    for i in range(len(HOPS)):
-        go(remote(line.at[0:4], asked.at[i], qs.at[i], qr.at[i], nears[i]))
 
     for copy in fetches:
         copy.start()
@@ -315,21 +329,26 @@
             radial[b, i] = values * curve
         return carry
 
-    def fill(slot, asked_line):
-        column = jnp.broadcast_to(asked_line, (128, 128)).T
-
-        def one(t, carry):
-            r = lax.rem(t // NX + ny - y, ny)
-            wanted = metas[r, t % NX, 0:1, :]
-            same = jnp.where(column == wanted, 1.0, 0.0).astype(F32)
-            hot[t, slot * 128 : (slot + 1) * 128, :] = same.astype(BF)
-            return carry
-
-        lax.fori_loop(0, devs, one, 0)
+    def fill(h):
+        def each(dx, carry):
+            xx = lax.rem(x + dx, NX)
+            asked_line = metas[0, xx, 0:1, :] if h == 0 else asked[h - 1, xx, 0:1, :]
+            column = jnp.broadcast_to(asked_line, (128, 128)).T
+
+            def one(rho, inner):
+                same = jnp.where(column == metas[rho, x, 0:1, :], 1.0, 0.0).astype(F32)
+                hot[rho, pl.ds((h * NX + dx) * 128, 128), :] = same.astype(BF)
+                return inner
+
+            return lax.fori_loop(0, ny, one, carry)
+
+        lax.fori_loop(0, NX, each, 0)
 
     for c in range(CHUNKS):
         process(0, c, (0, 1))
     row_meta(2)
+    for i in range(len(HOPS)):
+        go(remote(metas.at[0], asked.at[i], qs.at[i], qr.at[i], nears[i]))
     go(remote(metas.at[0], metas.at[1], ms.at[base], mr.at[base], down))
     go(remote(metas.at[0], metas.at[ny - 1], ms.at[base + far], mr.at[base + far], up))
     for c in range(CHUNKS):
@@ -385,13 +404,13 @@
         else:
             across_in(s - 1)
     for i in range(len(HOPS)):
-        remote(line.at[0:4], asked.at[i], qs.at[i], qr.at[i], nears[0]).wait_recv()
-    fill(0, metas[0, x, 0:1, :])
-    fill(1, asked[0, 0:1, :])
+        remote(metas.at[0], asked.at[i], qs.at[i], qr.at[i], nears[0]).wait_recv()
+    fill(0)
+    fill(1)
     for c in range(CHUNKS):
         passing(ny - 1, c)
     for i in range(1, len(HOPS)):
-        fill(1 + i, asked[i, 0:1, :])
+        fill(1 + i)
     across_in(far)
     for g in range(ny):
         row = row_of(g) * NX
@@ -436,54 +455,42 @@
     packed[0:8] = top
     packed[8:16] = low
 
-    sides = [{"dev": y * NX + (x + s) % NX} for s in range(1, NX)]
     for i in range(ny - 1):
-        go(remote(packed, every.at[y, x], ts.at[i], tr.at[i], ups[i]))
-    for i in range(NX - 1):
-        go(remote(packed, every.at[y, x], xs.at[0, i], xr_.at[0, i], sides[i]))
-    every[y, x] = packed[...]
-    near_first = sorted(range(1, ny), key=lambda j: min(j, ny - j))
-
-    def spread(j):
-        yy = (y + ny - j) % ny
-        remote(packed, every.at[yy, x], ts.at[j - 1], tr.at[j - 1], up).wait_recv()
-        for i in range(NX - 1):
-            go(remote(every.at[yy, x], every.at[yy, x], xs.at[j, i], xr_.at[j, i], sides[i]))
-
+        go(remote(packed, every.at[i + 1], ts.at[i], tr.at[i], ups[i]))
+    every[0] = packed[...]
+    turns = [0] + sorted(range(1, ny), key=lambda j: min(j, ny - j))
     sums[...] = jnp.zeros_like(sums)
-
-    def collect(j):
-        yy = (y + ny - j) % ny
-        for i in range(NX - 1):
-            xx = (x + NX - 1 - i) % NX
-            remote(packed, every.at[yy, xx], xs.at[j, i], xr_.at[j, i], right).wait_recv()
-        for pair in range(NX // 2):
-            lefts, rights = [], []
-            for xx in (2 * pair, 2 * pair + 1):
-                value = unpack(every[yy, xx, 0:8], every[yy, xx, 8:16], pairs)
-                high = value.astype(BF)
-                lowp = (value - high.astype(F32)).astype(BF)
-                lefts.append(jnp.concatenate([high, lowp], axis=0))
-                rights.append(hot[yy * NX + xx])
-            sums[...] += lax.dot_general(
-                jnp.concatenate(lefts, axis=1), jnp.concatenate(rights, axis=1), NT, preferred_element_type=F32
-            )
-
-    for j in near_first:
-        spread(j)
-    collect(0)
-    for j in near_first:
-        collect(j)
-    both = sums[0:32, :] + sums[32:64, :]
-    for i in range(len(HOPS)):
-        answer[i] = both[:, 128 * (i + 1) : 128 * (i + 2)]
-    for i in range(len(HOPS)):
-        back = {"region": (region - HOPS[i] + regions) % regions}
-        go(remote(answer.at[i], got.at[i], zs.at[i], zr.at[i], back))
-    moment = both[:, 0:128]
-    for i in range(len(HOPS)):
-        remote(answer.at[i], got.at[i], zs.at[i], zr.at[i], nears[0]).wait_recv()
-        moment = moment + got[i]
+    for pair in range(ny // 2):
+        lefts, rights = [], []
+        for j in turns[2 * pair : 2 * pair + 2]:
+            if j:
+                remote(packed, every.at[j], ts.at[j - 1], tr.at[j - 1], up).wait_recv()
+            value = unpack(every[j, 0:8], every[j, 8:16], pairs)
+            high = value.astype(BF)
+            rest = (value - high.astype(F32)).astype(BF)
+            lefts.append(jnp.concatenate([high, rest], axis=0))
+            rights.append(hot[(ny - j) % ny])
+        sums[...] += lax.dot_general(
+            jnp.concatenate(lefts, axis=1), jnp.concatenate(rights, axis=1), NT, preferred_element_type=F32
+        )
+
+    def answers_of(slot):
+        lanes = slice(128 * slot, 128 * (slot + 1))
+        return pack_sums(sums[0:32, lanes] + sums[32:64, lanes])
+
+    far_first = sorted(range(1, NX * (1 + len(HOPS))), key=lambda n: -(min(n % NX, NX - n % NX) + (n >= NX)))
+    for slot in far_first:
+        h, dx = slot // NX, slot % NX
+        answer[slot] = answers_of(slot)
+        where = {"dev": y * NX + (x + dx) % NX}
+        if h:
+            where["region"] = (region - HOPS[h - 1] + regions) % regions
+        go(remote(answer.at[slot], got.at[slot], zs.at[slot], zr.at[slot], where))
+    gained = answers_of(0)
+    for slot in reversed(far_first):
+        remote(answer.at[slot], got.at[slot], zs.at[slot], zr.at[slot], right).wait_recv()
+        gained = gained + got[slot]
+    moment = unpack_sums(gained)
     upright = jnp.concatenate([moment, jnp.zeros((96, 128), F32)], axis=0).T
     mom_ref[...] = upright[pairs : pairs + ATOM_DEV, 0:comps]
     for b in range(batches):
@@ -563,18 +570,18 @@
             pltpu.VMEM((devs,) + block, BF),
             pltpu.VMEM((8, 128), jnp.int32),
             pltpu.VMEM((ny, NX, 4, 128), jnp.int32),
-            pltpu.VMEM((hops, 4, 128), jnp.int32),
+            pltpu.VMEM((hops, NX, 4, 128), jnp.int32),
             pltpu.VMEM(basis_values.shape, BF),
             pltpu.VMEM(harmonics.shape, BF),
             pltpu.VMEM((batches, band * size, points), BF),
             pltpu.VMEM((batches, near, comps, points), F32),
             pltpu.VMEM((batches, near, comps, points), F32),
             pltpu.VMEM((16, 128), F32),
-            pltpu.VMEM((ny, NX, 16, 128), F32),
-            pltpu.VMEM((devs, 128 * (1 + hops), 128), BF),
-            pltpu.VMEM((64, 128 * (1 + hops)), F32),
-            pltpu.VMEM((hops, 32, 128), F32),
-            pltpu.VMEM((hops, 32, 128), F32),
+            pltpu.VMEM((ny, 16, 128), F32),
+            pltpu.VMEM((ny, 128 * NX * (1 + hops), 128), BF),
+            pltpu.VMEM((64, 128 * NX * (1 + hops)), F32),
+            pltpu.VMEM((NX * (1 + hops), 24, 128), F32),
+            pltpu.VMEM((NX * (1 + hops), 24, 128), F32),
             dma((ny - 1, CHUNKS)),
             dma((ny - 1, CHUNKS)),
             dma((ny + 3,)),
@@ -595,10 +602,8 @@
             dma((ny - 1,)),
             dma((ny - 1,)),
             dma((ny - 1,)),
-            dma((ny, NX - 1)),
-            dma((ny, NX - 1)),
-            dma((hops,)),
-            dma((hops,)),
+            dma((NX * (1 + hops),)),
+            dma((NX * (1 + hops),)),
             dma((5,)),
         ],
         compiler_params=pltpu.CompilerParams(collective_id=0, has_side_effects=True),

time: 83.4 us -> 81.3 us (0.975)
  Pallas kernels: 81.2 us -> 79.1 us
    pallas_call x1, Pallas kernels: 79.9 us -> 77.8 us  [per_device(): pl.pallas_call(functools.partial(kernel, ny), name='whole_step', out_shap...]
where the time goes in v5:
time: 81.3 us; the launch traced here: 80.4 us
  Pallas kernels  79.1 us (97%)
  between operations  1.29 us (2%)
    pallas_call x1, Pallas kernels, per_device(): pl.pallas_call(functools.partial(kernel, ny), name='whole_step', out_shap...  77.8 us

profile of v5, /device:TPU:6, one launch (start us, length us, event | category | flops | bytes accessed | tf_op | source)
XLA Modules:
  0.0 80.4 jit_solution(16217855276482138961)
XLA Ops:
  1.3 77.8 %whole_step.1 = (f32[12,256]{1,0:T(8,128)}, f32[16,25]{1,0:T(8,128)}, f32[12,256]{1,0:T(8,128)}) custom-call(bf16[3,4,128,128]{3,2,1,0:T(8,128)(2,1)} %rows_hbm.1, s32[3,4]{1,0:T(4,128)} %mask_ref.1, s32[1]{0:T(128)S(6)} %copy.14.start_ref, s32[1,12]{1,0:T(1,128)} %offsets_ref.1, s32[1,12]{1,0:T(1,128)} %sizes_ref.1, s32[6,12]{1,0:T(8,128)} %bitcast.4, ...), custom_call_target="tpu_custom_call" | custom-call | tf_op jit(solution)/shard_map/whole_step/pallas_call | solution.py:548
  79.0 1.4 %hand_over.1 = (f32[12,256]{1,0:T(8,128)}, f32[16,25]{1,0:T(8,128)}, f32[12,256]{1,0:T(8,128)}) custom-call(f32[12,256]{1,0:T(8,128)} %get-tuple-element.9.refs_0_, f32[16,25]{1,0:T(8,128)} %get-tuple-element.10.refs_1_, f32[12,256]{1,0:T(8,128)} %get-tuple-element.11.refs_2_), custom_call_target="tpu_custom_call" | custom-call | tf_op jit(solution)/shard_map/hand_over/pallas_call | solution.py:513

commit v6 on v5

--- a/solution.py
+++ b/solution.py
@@ -12,7 +12,6 @@
 CHUNKS = 2
 HOPS = (1, 2, -1, -2)
 MESH = pl.DeviceIdType.MESH
-NT = (((1,), (1,)), ((), ()))
 TN = (((0,), (0,)), ((), ()))
 F32, BF = jnp.float32, jnp.bfloat16
 
@@ -329,20 +328,19 @@
             radial[b, i] = values * curve
         return carry
 
-    def fill(h):
-        def each(dx, carry):
-            xx = lax.rem(x + dx, NX)
-            asked_line = metas[0, xx, 0:1, :] if h == 0 else asked[h - 1, xx, 0:1, :]
-            column = jnp.broadcast_to(asked_line, (128, 128)).T
-
-            def one(rho, inner):
-                same = jnp.where(column == metas[rho, x, 0:1, :], 1.0, 0.0).astype(F32)
-                hot[rho, pl.ds((h * NX + dx) * 128, 128), :] = same.astype(BF)
-                return inner
-
-            return lax.fori_loop(0, ny, one, carry)
-
-        lax.fori_loop(0, NX, each, 0)
+    def fill(some):
+        def one(rho, carry):
+            column = jnp.broadcast_to(metas[rho, x, 0:1, :], (128, 128)).T
+            for h in some:
+                for dx in range(NX):
+                    xx = (x + dx) % NX
+                    line_of = metas[0, xx, 0:1, :] if h == 0 else asked[h - 1, xx, 0:1, :]
+                    same = jnp.where(column == line_of, 1.0, 0.0).astype(F32)
+                    slot = h * NX + dx
+                    hot[rho, :, 128 * slot : 128 * (slot + 1)] = same.astype(BF)
+            return carry
+
+        lax.fori_loop(0, ny, one, 0)
 
     for c in range(CHUNKS):
         process(0, c, (0, 1))
@@ -405,12 +403,10 @@
             across_in(s - 1)
     for i in range(len(HOPS)):
         remote(metas.at[0], asked.at[i], qs.at[i], qr.at[i], nears[0]).wait_recv()
-    fill(0)
-    fill(1)
+    fill((0, 1))
     for c in range(CHUNKS):
         passing(ny - 1, c)
-    for i in range(1, len(HOPS)):
-        fill(1 + i)
+    fill(tuple(range(2, 1 + len(HOPS))))
     across_in(far)
     for g in range(ny):
         row = row_of(g) * NX
@@ -450,16 +446,18 @@
             gained = jnp.where(spot == i * batches + b, column, gained)
         return gained
 
-    terms = lax.fori_loop(0, batches, batch, jnp.zeros((comps, 128), F32), unroll=4)
+    terms = lax.fori_loop(0, batches, batch, jnp.zeros((comps, 128), F32), unroll=True)
     top, low = pack(terms, pairs)
     packed[0:8] = top
     packed[8:16] = low
 
-    for i in range(ny - 1):
+    early = list(started)
+    for i in sorted(range(ny - 1), key=lambda i: -min(i + 1, ny - i - 1)):
         go(remote(packed, every.at[i + 1], ts.at[i], tr.at[i], ups[i]))
     every[0] = packed[...]
+    for copy in early:
+        copy.wait_send()
     turns = [0] + sorted(range(1, ny), key=lambda j: min(j, ny - j))
-    sums[...] = jnp.zeros_like(sums)
     for pair in range(ny // 2):
         lefts, rights = [], []
         for j in turns[2 * pair : 2 * pair + 2]:
@@ -470,9 +468,12 @@
             rest = (value - high.astype(F32)).astype(BF)
             lefts.append(jnp.concatenate([high, rest], axis=0))
             rights.append(hot[(ny - j) % ny])
-        sums[...] += lax.dot_general(
-            jnp.concatenate(lefts, axis=1), jnp.concatenate(rights, axis=1), NT, preferred_element_type=F32
+        gain = jnp.dot(
+            jnp.concatenate(lefts, axis=1), jnp.concatenate(rights, axis=0), preferred_element_type=F32
         )
+        if pair:
+            gain = gain + sums[...]
+        sums[...] = gain
 
     def answers_of(slot):
         lanes = slice(128 * slot, 128 * (slot + 1))
@@ -500,7 +501,7 @@
             gathered = gathered + radial[b, i] * moment[0:comps, q : q + 1]
         value = jnp.sum(gathered, axis=0, keepdims=True)
         pot_ref[b : b + 1, :] = jnp.where(wide < sizes_ref[0, b], value, 0.0)
-    for copy in started:
+    for copy in started[len(early) :]:
         copy.wait_send()
 
 
@@ -578,7 +579,7 @@
             pltpu.VMEM((batches, near, comps, points), F32),
             pltpu.VMEM((16, 128), F32),
             pltpu.VMEM((ny, 16, 128), F32),
-            pltpu.VMEM((ny, 128 * NX * (1 + hops), 128), BF),
+            pltpu.VMEM((ny, 128, 128 * NX * (1 + hops)), BF),
             pltpu.VMEM((64, 128 * NX * (1 + hops)), F32),
             pltpu.VMEM((NX * (1 + hops), 24, 128), F32),
             pltpu.VMEM((NX * (1 + hops), 24, 128), F32),

time: 81.3 us -> 80.2 us (0.986)
  Pallas kernels: 79.1 us -> 77.9 us
    pallas_call x1, Pallas kernels: 77.8 us -> 76.5 us  [per_device(): pl.pallas_call(functools.partial(kernel, ny), name='whole_step', out_shap...]
where the time goes in v6:
time: 80.2 us; the launch traced here: 79.2 us
  Pallas kernels  77.9 us (97%)
  between operations  1.29 us (2%)
    pallas_call x1, Pallas kernels, per_device(): pl.pallas_call(functools.partial(kernel, ny), name='whole_step', out_shap...  76.5 us

profile of v6, /device:TPU:6, one launch (start us, length us, event | category | flops | bytes accessed | tf_op | source)
XLA Modules:
  0.0 79.2 jit_solution(12941175877986612316)
XLA Ops:
  1.3 76.5 %whole_step.1 = (f32[12,256]{1,0:T(8,128)}, f32[16,25]{1,0:T(8,128)}, f32[12,256]{1,0:T(8,128)}) custom-call(bf16[3,4,128,128]{3,2,1,0:T(8,128)(2,1)} %rows_hbm.1, s32[3,4]{1,0:T(4,128)} %mask_ref.1, s32[1]{0:T(128)S(6)} %copy.14.start_ref, s32[1,12]{1,0:T(1,128)} %offsets_ref.1, s32[1,12]{1,0:T(1,128)} %sizes_ref.1, s32[6,12]{1,0:T(8,128)} %bitcast.4, ...), custom_call_target="tpu_custom_call" | custom-call | tf_op jit(solution)/shard_map/whole_step/pallas_call | solution.py:549
  77.8 1.4 %hand_over.1 = (f32[12,256]{1,0:T(8,128)}, f32[16,25]{1,0:T(8,128)}, f32[12,256]{1,0:T(8,128)}) custom-call(f32[12,256]{1,0:T(8,128)} %get-tuple-element.9.refs_0_, f32[16,25]{1,0:T(8,128)} %get-tuple-element.10.refs_1_, f32[12,256]{1,0:T(8,128)} %get-tuple-element.11.refs_2_), custom_call_target="tpu_custom_call" | custom-call | tf_op jit(solution)/shard_map/hand_over/pallas_call | solution.py:514

commit v7 on v6

--- a/solution.py
+++ b/solution.py
@@ -506,17 +506,24 @@
 
 
 def hand_over(*arrays):
+    count = len(arrays)
+
     def copies(*refs):
-        for source, target in zip(refs[: len(arrays)], refs[len(arrays) :]):
-            target[...] = source[...]
-
-    vm = pl.BlockSpec(memory_space=pltpu.VMEM)
+        sems = refs[2 * count]
+        moves = [pltpu.make_async_copy(refs[n], refs[count + n], sems.at[n]) for n in range(count)]
+        for move in moves:
+            move.start()
+        for move in moves:
+            move.wait()
+
+    hb = pl.BlockSpec(memory_space=pl.ANY)
     return pl.pallas_call(
         copies,
         name="hand_over",
         out_shape=tuple(jax.ShapeDtypeStruct(a.shape, a.dtype) for a in arrays),
-        in_specs=[vm] * len(arrays),
-        out_specs=(vm,) * len(arrays),
+        in_specs=[hb] * count,
+        out_specs=(hb,) * count,
+        scratch_shapes=[pltpu.SemaphoreType.DMA((count,))],
     )(*arrays)
 
 

time: 80.2 us -> 81.1 us (1.011)
  Pallas kernels: 77.9 us -> 78.9 us
    pallas_call x1, Pallas kernels: 1.37 us -> 2.37 us  [hand_over(): pl.pallas_call(copies, name='hand_over', out_shape=tuple((jax.ShapeDtypeS...]
where the time goes in v7:
time: 81.1 us; the launch traced here: 80.2 us
  Pallas kernels  78.9 us (97%)
  between operations  1.29 us (2%)
    pallas_call x1, Pallas kernels, per_device(): pl.pallas_call(functools.partial(kernel, ny), name='whole_step', out_shap...  76.5 us
    pallas_call x1, Pallas kernels, hand_over(): pl.pallas_call(copies, name='hand_over', out_shape=tuple((jax.ShapeDtypeS...  2.37 us

profile of v7, /device:TPU:6, one launch (start us, length us, event | category | flops | bytes accessed | tf_op | source)
XLA Modules:
  0.0 80.2 jit_solution(3071498077679160723)
XLA Ops:
  1.3 76.5 %whole_step.1 = (f32[12,256]{1,0:T(8,128)}, f32[16,25]{1,0:T(8,128)}, f32[12,256]{1,0:T(8,128)}) custom-call(bf16[3,4,128,128]{3,2,1,0:T(8,128)(2,1)} %rows_hbm.1, s32[3,4]{1,0:T(4,128)} %mask_ref.1, s32[1]{0:T(128)S(6)} %copy.14.start_ref, s32[1,12]{1,0:T(1,128)} %offsets_ref.1, s32[1,12]{1,0:T(1,128)} %sizes_ref.1, s32[6,12]{1,0:T(8,128)} %bitcast.4, ...), custom_call_target="tpu_custom_call" | custom-call | tf_op jit(solution)/shard_map/whole_step/pallas_call | solution.py:556
  77.8 2.4 %hand_over.1 = (f32[12,256]{1,0:T(8,128)}, f32[16,25]{1,0:T(8,128)}, f32[12,256]{1,0:T(8,128)}) custom-call(f32[12,256]{1,0:T(8,128)} %get-tuple-element.9.refs_0_, f32[16,25]{1,0:T(8,128)} %get-tuple-element.10.refs_1_, f32[12,256]{1,0:T(8,128)} %get-tuple-element.11.refs_2_), custom_call_target="tpu_custom_call" | custom-call | tf_op jit(solution)/shard_map/hand_over/pallas_call | solution.py:520
